TPU v7x, 32 devices: a whole 2x2x4 slice. The times are simulated.
32 devices in a mesh: wide: 8 (over z, y), narrow: 4 (over x, core).
Axes of the slice: x: 2, y: 2, z: 4, core: 2. Of those that a mesh axis runs over, the one named last changes fastest.
Arguments:
- tokens: bfloat16 [4096, 2048], P('wide'), may hold values from -6 to 6
- cotangent: bfloat16 [4096, 2048], P('wide'), may hold values from -6 to 6
- keep_mask: int32 [4096], P('wide'), may hold values 0 or 1
- doc_lengths: int32 [1, 16], replicated, may hold values from 1 to 2048, 4096 in all within a row
- block_order: int32 [1, 16], replicated, may hold values from 0 to 15, each once within a row
- gain_attn: bfloat16 [2048], replicated, may hold values from 0.25 to 1.75
- w_query: bfloat16 [2048, 2048], P(None, 'narrow'), may hold values from -0.125 to 0.125
- w_key: bfloat16 [2048, 1024], P(None, 'narrow'), may hold values from -0.125 to 0.125
- w_value: bfloat16 [2048, 1024], P(None, 'narrow'), may hold values from -0.125 to 0.125
- w_out: bfloat16 [2048, 2048], P('narrow'), may hold values from -0.5 to 0.5
- gain_dense: bfloat16 [2048], replicated, may hold values from 0.25 to 1.75
- w_gate: bfloat16 [2048, 5632], P(None, 'narrow'), may hold values from -0.125 to 0.125
- w_up: bfloat16 [2048, 5632], P(None, 'narrow'), may hold values from -0.125 to 0.125
- w_down: bfloat16 [5632, 2048], P('narrow'), may hold values from -0.078125 to 0.078125
Outputs:
- output: bfloat16 [4096, 2048], P('wide')
- grad_tokens: bfloat16 [4096, 2048], P('wide')
- grad_gain_attn: float32 [2048], P('wide')
- grad_w_query: float32 [2048, 2048], P('wide', 'narrow')
- grad_w_key: float32 [2048, 1024], P('wide', 'narrow')
- grad_w_value: float32 [2048, 1024], P('wide', 'narrow')
- grad_w_out: float32 [2048, 2048], P('narrow', 'wide')
- grad_gain_dense: float32 [2048], P('wide')
- grad_w_gate: float32 [2048, 5632], P('wide', 'narrow')
- grad_w_up: float32 [2048, 5632], P('wide', 'narrow')
- grad_w_down: float32 [5632, 2048], P('narrow', 'wide')
All inputs are finite; a program needn't handle non-finite values. No bound on the sum of `keep_mask` on one device may be relied on, other than what follows from the above.
Results may differ from a plain program's by a relative error of at most 0.025.
Values may be sent and summed in bfloat16 or wider, within the bound.
No kernel may reach another device: no remote copies, remote signals or barrier semaphores. Data moves between devices by JAX's collectives and lax.ppermute only.
A program may use at most 192 MiB of HBM per device.

v0:
```python
import jax
import jax.numpy as jnp
from jax import lax
from jax.sharding import PartitionSpec as P

HD = 128
LOG_DEVS = 3


EPSILON = 1e-05
NEGATIVE = -1e30
BASE = 10000.0


def swapped(value, axis, stride):
    mask = 2**stride
    pairs = [(source, source ^ mask) for source in range(lax.axis_size(axis))]
    return lax.ppermute(value, axis, pairs)


def rms_scale(values):
    return lax.rsqrt(jnp.mean(values * values, axis=1, keepdims=True) + EPSILON)


def rotary_tables(positions, head_size):
    halfway = head_size // 2
    frequency = BASE ** (-(jnp.arange(halfway, dtype=jnp.float32) * 2.0) / head_size)
    angles = positions.astype(jnp.float32)[:, None] * frequency[None, :]
    return (jnp.cos(angles), jnp.sin(angles))


def rotate(values, cosine, sine_table):
    halfway = values.shape[-1] // 2
    leading = values[..., :halfway]
    trailing = values[..., halfway:]
    cosine = cosine[:, None, :]
    sine_table = sine_table[:, None, :]
    return jnp.concatenate(
        [leading * cosine - trailing * sine_table, trailing * cosine + leading * sine_table],
        axis=-1,
    )


def norm_backward(source, scale_rows, gain, upstream):
    weighted = upstream * gain
    average = jnp.mean(weighted * source, axis=1, keepdims=True)
    return scale_rows * weighted - source * scale_rows**3 * average


def group_gather(rows, member):
    buffer = rows
    for level in range(LOG_DEVS):
        other = swapped(buffer, "wide", level)
        lower_side = member // (1 << level) % 2 == 0
        buffer = jnp.where(
            lower_side,
            jnp.concatenate([buffer, other], axis=0),
            jnp.concatenate([other, buffer], axis=0),
        )
    return buffer


def group_gather_again(rows, member):
    buffer = rows
    for level in range(LOG_DEVS):
        other = swapped(buffer, "wide", level)
        lower_side = member // (1 << level) % 2 == 0
        buffer = jnp.where(
            lower_side,
            jnp.concatenate([buffer, other], axis=0),
            jnp.concatenate([other, buffer], axis=0),
        )
    return buffer


def group_reduce(terms, member):
    buffer = terms
    for level in reversed(range(LOG_DEVS)):
        halfway = buffer.shape[0] // 2
        lower_part = buffer[:halfway]
        upper_part = buffer[halfway:]
        upper_side = member // (1 << level) % 2 == 1
        kept_part = jnp.where(upper_side, upper_part, lower_part)
        sent_part = jnp.where(upper_side, lower_part, upper_part)
        buffer = kept_part + swapped(sent_part.astype(jnp.bfloat16), "wide", level).astype(
            sent_part.dtype
        )
    return buffer


def shards(
    tokens,
    cotangent,
    keep_mask,
    doc_lengths,
    block_order,
    gain_attn,
    w_query,
    w_key,
    w_value,
    w_out,
    gain_dense,
    w_gate,
    w_up,
    w_down,
):
    local_rows = tokens.shape[0]
    group_size = 2**LOG_DEVS
    seq_rows = local_rows * group_size
    half_rows = local_rows // 2
    q_heads = w_query.shape[1] // HD
    kv_heads = w_key.shape[1] // HD
    kv_width = kv_heads * HD
    grouped = q_heads // kv_heads
    factor = HD ** (-0.5)
    block_rows = min(1024, seq_rows)
    block_count = seq_rows // block_rows
    wide_index = lax.axis_index("wide")
    seq_index = wide_index // group_size
    member = wide_index % group_size
    order_row = lax.dynamic_index_in_dim(block_order, seq_index, 0, keepdims=False)
    length_row = lax.dynamic_index_in_dim(doc_lengths, seq_index, 0, keepdims=False)
    positions_seq = (
        order_row[:, None] * half_rows + jnp.arange(half_rows, dtype=jnp.int32)[None, :]
    ).reshape(-1)
    doc_ends = jnp.cumsum(length_row)
    documents_seq = jnp.sum((doc_ends[None, :] <= positions_seq[:, None]).astype(jnp.int32), axis=1)
    first_row = member * local_rows
    positions = lax.dynamic_slice_in_dim(positions_seq, first_row, local_rows)
    documents = lax.dynamic_slice_in_dim(documents_seq, first_row, local_rows)
    cosine, sine_table = rotary_tables(positions, HD)
    source = tokens.astype(jnp.float32)
    keep_rows = keep_mask.astype(jnp.float32)[:, None]
    gain_one = gain_attn.astype(jnp.float32)
    scale_one = rms_scale(source)
    normed_one = (source * scale_one * gain_one).astype(jnp.bfloat16)
    query_raw = jnp.dot(normed_one, w_query, preferred_element_type=jnp.float32)
    key_raw = jnp.dot(normed_one, w_key, preferred_element_type=jnp.float32)
    value_rows = jnp.dot(normed_one, w_value, preferred_element_type=jnp.float32).astype(
        jnp.bfloat16
    )
    query_rot = (
        rotate(query_raw.reshape(local_rows, q_heads, HD), cosine, sine_table)
        .astype(jnp.bfloat16)
        .reshape(local_rows, kv_heads, grouped, HD)
    )
    key_rows = (
        rotate(key_raw.reshape(local_rows, kv_heads, HD), cosine, sine_table)
        .astype(jnp.bfloat16)
        .reshape(local_rows, kv_width)
    )
    both_rows = jnp.concatenate([key_rows, value_rows], axis=1)
    both_all = group_gather(both_rows, member)
    keys_all = both_all[:, :kv_width]
    values_all = both_all[:, kv_width:]

    def allowed_block(first_key):
        key_pos = lax.dynamic_slice_in_dim(positions_seq, first_key, block_rows)
        key_doc = lax.dynamic_slice_in_dim(documents_seq, first_key, block_rows)
        return (key_pos[None, :] <= positions[:, None]) & (key_doc[None, :] == documents[:, None])

    def scores_block(keys_source, first_key):
        key_block = lax.dynamic_slice_in_dim(keys_source, first_key, block_rows).reshape(
            block_rows, kv_heads, HD
        )
        raw_scores = (
            jnp.einsum("tgrd,kgd->grtk", query_rot, key_block, preferred_element_type=jnp.float32)
            * factor
        )
        return (jnp.where(allowed_block(first_key)[None, None], raw_scores, NEGATIVE), key_block)

    def gather_stats(state, block_index):
        running, summed = state
        scores, unused = scores_block(keys_all, block_index * block_rows)
        peak_score = jnp.maximum(running, jnp.max(scores, axis=-1))
        summed = summed * jnp.exp(running - peak_score) + jnp.sum(
            jnp.exp(scores - peak_score[..., None]), axis=-1
        )
        return ((peak_score, summed), None)

    stat_shape = (kv_heads, grouped, local_rows)
    start_stats = (jnp.full(stat_shape, NEGATIVE, jnp.float32), jnp.zeros(stat_shape, jnp.float32))
    (running, summed), unused = lax.scan(gather_stats, start_stats, jnp.arange(block_count))
    log_total = running + jnp.log(summed)

    def weigh_values(running_sum, block_index):
        first_key = block_index * block_rows
        scores, unused = scores_block(keys_all, first_key)
        weights_low = jnp.exp(scores - log_total[..., None]).astype(jnp.bfloat16)
        value_block = lax.dynamic_slice_in_dim(values_all, first_key, block_rows).reshape(
            block_rows, kv_heads, HD
        )
        return (
            running_sum
            + jnp.einsum(
                "grtk,kgd->tgrd", weights_low, value_block, preferred_element_type=jnp.float32
            ),
            None,
        )

    mixed_exact, unused = lax.scan(
        weigh_values,
        jnp.zeros((local_rows, kv_heads, grouped, HD), jnp.float32),
        jnp.arange(block_count),
    )
    mixed_heads = mixed_exact.astype(jnp.bfloat16).reshape(local_rows, q_heads * HD)
    attn_out = lax.psum(
        jnp.dot(mixed_heads, w_out, preferred_element_type=jnp.float32).astype(jnp.bfloat16),
        "narrow",
    ).astype(jnp.float32)
    hidden_one = source + keep_rows * attn_out
    gain_two = gain_dense.astype(jnp.float32)
    scale_two = rms_scale(hidden_one)
    normed_two = (hidden_one * scale_two * gain_two).astype(jnp.bfloat16)
    gate_proj = jnp.dot(normed_two, w_gate, preferred_element_type=jnp.float32)
    up_proj = jnp.dot(normed_two, w_up, preferred_element_type=jnp.float32)
    sigmoid_gate = jax.nn.sigmoid(gate_proj)
    activated = gate_proj * sigmoid_gate
    inner_act = (activated * up_proj).astype(jnp.bfloat16)
    dense_out = lax.psum(
        jnp.dot(inner_act, w_down, preferred_element_type=jnp.float32).astype(jnp.bfloat16),
        "narrow",
    ).astype(jnp.float32)
    output = (hidden_one + keep_rows * dense_out).astype(jnp.bfloat16)
    upstream = cotangent.astype(jnp.float32)
    d_dense = (keep_rows * upstream).astype(jnp.bfloat16)
    d_inner = jnp.dot(d_dense, w_down.T, preferred_element_type=jnp.float32)
    d_gate = (d_inner * up_proj * sigmoid_gate * (1.0 + gate_proj * (1.0 - sigmoid_gate))).astype(
        jnp.bfloat16
    )
    d_up = (d_inner * activated).astype(jnp.bfloat16)
    d_normed_two = lax.psum(
        (
            jnp.dot(d_gate, w_gate.T, preferred_element_type=jnp.float32)
            + jnp.dot(d_up, w_up.T, preferred_element_type=jnp.float32)
        ).astype(jnp.bfloat16),
        "narrow",
    ).astype(jnp.float32)
    grad_gate = jnp.dot(normed_two.T, d_gate, preferred_element_type=jnp.float32)
    grad_up = jnp.dot(normed_two.T, d_up, preferred_element_type=jnp.float32)
    grad_down = jnp.dot(inner_act.T, d_dense, preferred_element_type=jnp.float32)
    grad_gate, grad_up, grad_down = (
        lax.psum_scatter(
            grad_gate.astype(jnp.bfloat16), "wide", scatter_dimension=0, tiled=True
        ).astype(jnp.float32),
        lax.psum_scatter(
            grad_up.astype(jnp.bfloat16), "wide", scatter_dimension=0, tiled=True
        ).astype(jnp.float32),
        lax.psum_scatter(
            grad_down.astype(jnp.bfloat16), "wide", scatter_dimension=1, tiled=True
        ).astype(jnp.float32),
    )
    grad_gain_two = jnp.sum(d_normed_two * hidden_one * scale_two, axis=0)
    d_hidden = upstream + norm_backward(hidden_one, scale_two, gain_two, d_normed_two)
    d_attn = (keep_rows * d_hidden).astype(jnp.bfloat16)
    grad_out_proj = jnp.dot(mixed_heads.T, d_attn, preferred_element_type=jnp.float32)
    d_mixed = (
        jnp.dot(d_attn, w_out.T, preferred_element_type=jnp.float32)
        .astype(jnp.bfloat16)
        .reshape(local_rows, kv_heads, grouped, HD)
    )
    row_delta = jnp.transpose(
        jnp.sum(d_mixed.astype(jnp.float32) * mixed_exact, axis=-1), (1, 2, 0)
    )
    both_back = group_gather_again(both_rows, member)
    keys_back = both_back[:, :kv_width]
    values_back = both_back[:, kv_width:]

    def backward_block(query_grad, block_index):
        first_key = block_index * block_rows
        scores, key_block = scores_block(keys_back, first_key)
        value_block = lax.dynamic_slice_in_dim(values_back, first_key, block_rows).reshape(
            block_rows, kv_heads, HD
        )
        weights_exact = jnp.exp(scores - log_total[..., None])
        weights_low = weights_exact.astype(jnp.bfloat16)
        value_grads = jnp.einsum(
            "grtk,tgrd->kgd", weights_low, d_mixed, preferred_element_type=jnp.float32
        )
        d_weights = jnp.einsum(
            "tgrd,kgd->grtk", d_mixed, value_block, preferred_element_type=jnp.float32
        )
        d_scores = (weights_exact * (d_weights - row_delta[..., None])).astype(jnp.bfloat16)
        query_grad = (
            query_grad
            + jnp.einsum("grtk,kgd->tgrd", d_scores, key_block, preferred_element_type=jnp.float32)
            * factor
        )
        key_grads = (
            jnp.einsum("grtk,tgrd->kgd", d_scores, query_rot, preferred_element_type=jnp.float32)
            * factor
        )
        return (query_grad, (key_grads, value_grads))

    d_query_rot, (key_parts, value_parts) = lax.scan(
        backward_block,
        jnp.zeros((local_rows, kv_heads, grouped, HD), jnp.float32),
        jnp.arange(block_count),
    )
    both_parts = jnp.concatenate(
        [key_parts.reshape(seq_rows, kv_width), value_parts.reshape(seq_rows, kv_width)], axis=1
    )
    both_grads = group_reduce(both_parts, member)
    d_keys = both_grads[:, :kv_width]
    d_values = both_grads[:, kv_width:]
    d_query_raw = (
        rotate(d_query_rot.reshape(local_rows, q_heads, HD), cosine, -sine_table)
        .astype(jnp.bfloat16)
        .reshape(local_rows, q_heads * HD)
    )
    d_key_raw = (
        rotate(d_keys.reshape(local_rows, kv_heads, HD), cosine, -sine_table)
        .astype(jnp.bfloat16)
        .reshape(local_rows, kv_width)
    )
    d_value_raw = d_values.astype(jnp.bfloat16)
    d_normed_one = lax.psum(
        (
            jnp.dot(d_query_raw, w_query.T, preferred_element_type=jnp.float32)
            + jnp.dot(d_key_raw, w_key.T, preferred_element_type=jnp.float32)
            + jnp.dot(d_value_raw, w_value.T, preferred_element_type=jnp.float32)
        ).astype(jnp.bfloat16),
        "narrow",
    ).astype(jnp.float32)
    grad_query = jnp.dot(normed_one.T, d_query_raw, preferred_element_type=jnp.float32)
    grad_key = jnp.dot(normed_one.T, d_key_raw, preferred_element_type=jnp.float32)
    grad_value = jnp.dot(normed_one.T, d_value_raw, preferred_element_type=jnp.float32)
    grad_gain_one = jnp.sum(d_normed_one * source * scale_one, axis=0)
    grad_tokens = (d_hidden + norm_backward(source, scale_one, gain_one, d_normed_one)).astype(
        jnp.bfloat16
    )
    grad_query, grad_key, grad_value, grad_out_proj, grad_gain_one, grad_gain_two = (
        lax.psum_scatter(
            grad_query.astype(jnp.bfloat16), "wide", scatter_dimension=0, tiled=True
        ).astype(jnp.float32),
        lax.psum_scatter(
            grad_key.astype(jnp.bfloat16), "wide", scatter_dimension=0, tiled=True
        ).astype(jnp.float32),
        lax.psum_scatter(
            grad_value.astype(jnp.bfloat16), "wide", scatter_dimension=0, tiled=True
        ).astype(jnp.float32),
        lax.psum_scatter(
            grad_out_proj.astype(jnp.bfloat16), "wide", scatter_dimension=1, tiled=True
        ).astype(jnp.float32),
        lax.psum_scatter(
            grad_gain_one.astype(jnp.bfloat16), "wide", scatter_dimension=0, tiled=True
        ).astype(jnp.float32),
        lax.psum_scatter(
            grad_gain_two.astype(jnp.bfloat16), "wide", scatter_dimension=0, tiled=True
        ).astype(jnp.float32),
    )
    return (
        output,
        grad_tokens,
        grad_gain_one,
        grad_query,
        grad_key,
        grad_value,
        grad_out_proj,
        grad_gain_two,
        grad_gate,
        grad_up,
        grad_down,
    )


def solution(mesh):
    placed = (
        P("wide", None),
        P("wide", None),
        P("wide"),
        P(),
        P(),
        P(),
        P(None, "narrow"),
        P(None, "narrow"),
        P(None, "narrow"),
        P("narrow", None),
        P(),
        P(None, "narrow"),
        P(None, "narrow"),
        P("narrow", None),
    )
    return jax.shard_map(
        shards,
        mesh=mesh,
        in_specs=placed,
        out_specs=(
            P("wide", None),
            P("wide", None),
            P("wide"),
            P("wide", "narrow"),
            P("wide", "narrow"),
            P("wide", "narrow"),
            P("narrow", "wide"),
            P("wide"),
            P("wide", "narrow"),
            P("wide", "narrow"),
            P("narrow", "wide"),
        ),
        check_vma=False,
    )
```

profile of v0, /device:TPU:0, one launch (start us, length us, event | category | flops | bytes accessed | tf_op | source)
XLA Modules:
  0.0 1295.1 jit_solution(13425788538345711609)
XLA Ops:
  24.1 12.0 collective-permute-done
  39.7 22.6 %collective-permute-done.1 = bf16[1024,512]{0,1:T(8,128)(2,1)} collective-permute-done((bf16[1024,512]{0,1:T(8,128)(2,1)S(1)}, bf16[1024,512]{0,1:T(8,128)(2,1)}, u32[]{:S(2)}, u32[]{:S(2)}) %collective-permute-start.1) | collective-permute-done | bytes 1048608 | tf_op jit(solution)/shard_map/ppermute | solution.py:18
  75.6 82.6 %collective-permute-done.2 = bf16[2048,512]{0,1:T(8,128)(2,1)} collective-permute-done((bf16[2048,512]{0,1:T(8,128)(2,1)}, bf16[2048,512]{0,1:T(8,128)(2,1)}, u32[]{:S(2)}, u32[]{:S(2)}) %collective-permute-start.2) | collective-permute-done | bytes 2097184 | tf_op jit(solution)/shard_map/ppermute | solution.py:18
  165.9 50.8 %while.39 = (s32[]{:T(128)}, f32[2,2,512]{2,1,0:T(2,128)S(1)}, f32[2,2,512]{2,1,0:T(2,128)S(1)}, s32[4]{0:T(128)S(1)}, s32[4096]{0:T(1024)S(1)}, /*index=5*/s32[...) while((s32[]{:T(128)}, f32[2,2,512]{2,1,0:T(2,128)S(1)}, ...), condition=%wide.region_6.7_spmd.clone, body=%wide.region_3.6_spmd.clone.sunk | while | flops 553134080 | bytes 20582612 | solution.py:183
  216.8 41.4 %while.40 = (s32[]{:T(128)}, f32[512,2,2,128]{0,3,2,1:T(8,128)}, s32[4]{0:T(128)S(1)}, bf16[4096,256]{0,1:T(8,128)(2,1)}, s32[4096]{0:T(1024)S(1)}, /*index=5*/s...) while((s32[]{:T(128)}, f32[512,2,2,128]{0,3,2,1:T(8,128)}, ...), condition=%wide.region_8.9_spmd.clone, body=%wide.region_7.8_spmd.clone.sunk | while | flops 1084227584 | bytes 6852829 | solution.py:201
  262.3 52.2 %all-reduce.8.cloned.1.call-done = bf16[512,2048]{1,0:T(8,128)(2,1)} async-done(((bf16[512,2048]{1,0:T(8,128)(2,1)}), bf16[512,2048]{1,0:T(8,128)(2,1)}) %all-reduce.8.cloned.1.call-update) | async-done | bytes 2097168 | tf_op jit(solution)/shard_map/psum | solution.py:207
  331.2 9.2 multiply_convert_fusion.2
  350.2 51.5 %all-reduce.10.cloned.1.call-done = bf16[512,2048]{1,0:T(8,128)(2,1)} async-done(((bf16[512,2048]{1,0:T(8,128)(2,1)}), bf16[512,2048]{1,0:T(8,128)(2,1)}) %all-reduce.10.cloned.1.call-update) | async-done | bytes 2097168 | tf_op jit(solution)/shard_map/psum | solution.py:232
  416.6 77.4 %while.41 = (s32[]{:T(128)}, f32[512,2,2,128]{0,3,2,1:T(8,128)}, f32[4,1024,2,128]{3,2,1,0:T(2,128)}, f32[4,1024,2,128]{3,2,1,0:T(2,128)}, s32[4]{0:T(128)S(1)},...) while((s32[]{:T(128)}, f32[512,2,2,128]{0,3,2,1:T(8,128)}, ...), condition=%wide.region_16.17_spmd.clone, body=%wide.region_15.16_spmd.clone.sunk | while | flops 2707947520 | bytes 70308632 | solution.py:295
  507.0 103.6 %collective-permute-done.3 = bf16[2048,512]{1,0:T(8,128)(2,1)} collective-permute-done((bf16[2048,512]{1,0:T(8,128)(2,1)}, bf16[2048,512]{1,0:T(8,128)(2,1)}, u32[]{:S(2)}, u32[]{:S(2)}) %collective-permute-start.3) | collective-permute-done | bytes 2097184 | tf_op jit(solution)/shard_map/ppermute | solution.py:18
  618.1 32.9 %collective-permute-done.4 = bf16[1024,512]{1,0:T(8,128)(2,1)} collective-permute-done((bf16[1024,512]{1,0:T(8,128)(2,1)S(1)}, bf16[1024,512]{1,0:T(8,128)(2,1)}, u32[]{:S(2)}, u32[]{:S(2)}) %collective-permute-start.4) | collective-permute-done | bytes 1048608 | tf_op jit(solution)/shard_map/ppermute | solution.py:18
  655.8 13.6 %collective-permute-done.5 = bf16[512,512]{1,0:T(8,128)(2,1)S(1)} collective-permute-done((bf16[512,512]{1,0:T(8,128)(2,1)S(1)}, bf16[512,512]{1,0:T(8,128)(2,1)S(1)}, u32[]{:S(2)}, u32[]{:S(2)}) %collective-permute-start.5) | collective-permute-done | bytes 524320 | tf_op jit(solution)/shard_map/ppermute | solution.py:18
  678.0 8.0 convolution_convert_fusion.6
  690.7 8.0 convolution_convert_fusion.2
  698.8 8.0 convolution_convert_fusion.1
  707.1 7.9 convolution_convert_fusion
  724.8 64.7 %reduce-scatter.10.cloned.1.call-done = bf16[256,256]{1,0:T(8,128)(2,1)} async-done(((bf16[2048,256]{1,0:T(8,128)(2,1)}), bf16[256,256]{1,0:T(8,128)(2,1)}) %reduce-scatter.10.cloned.1.call-update) | async-done | bytes 131088 | tf_op jit(solution)/shard_map/reduce_scatter | solution.py:336
  791.1 64.9 %reduce-scatter.12.cloned.1.call-done = bf16[256,256]{1,0:T(8,128)(2,1)} async-done(((bf16[2048,256]{1,0:T(8,128)(2,1)}), bf16[256,256]{1,0:T(8,128)(2,1)}) %reduce-scatter.12.cloned.1.call-update) | async-done | bytes 131088 | tf_op jit(solution)/shard_map/reduce_scatter | solution.py:339
  857.7 86.0 %all-reduce.12.cloned.1.call-done = (bf16[512,2048]{1,0:T(8,128)(2,1)}, bf16[512,2048]{1,0:T(8,128)(2,1)}) async-done(((bf16[512,2048]{1,0:T(8,128)(2,1)}, bf16[512,2048]{1,0:T(8,128)(2,1)}), (bf16[512,2048]{1,0:T(8,128)(2,1)}, bf16[512,2048]{1,0:T(8,128)(2,1)})) %all-reduce.12.cloned.1.call-update) | async-done | bytes 4194320 | tf_op jit(solution)/shard_map/psum | solution.py:220
  946.8 22.5 %all-reduce.2 = (bf16[2048]{0:T(1024)(128)(2,1)S(1)}, bf16[2048]{0:T(1024)(128)(2,1)S(1)}) all-reduce(bf16[2048]{0:T(1024)(128)(2,1)S(1)} %get-tuple-element.443, bf16[2048]{0:T(1024)(128)(2,1)S(1)} %copy-done.35), channel_id=2, replica_groups=mesh['wide'=8,'narrow'=4] {'wide'}, use_global_device_ids=true, to_apply=%region_20.21.clone | all-reduce | flops 4096 | bytes 16384
  969.9 7.7 fusion.41
  977.6 80.6 %reduce-scatter.16.cloned.1.call-done = bf16[256,1408]{1,0:T(8,128)(2,1)} async-done(((bf16[2048,1408]{1,0:T(8,128)(2,1)}), bf16[256,1408]{1,0:T(8,128)(2,1)}) %reduce-scatter.16.cloned.1.call-update) | async-done | bytes 720912 | tf_op jit(solution)/shard_map/reduce_scatter | solution.py:243
  1060.5 111.3 %reduce-scatter.18.cloned.1.call-done = bf16[256,1408]{1,0:T(8,128)(2,1)} async-done(((bf16[2048,1408]{1,0:T(8,128)(2,1)}), bf16[256,1408]{1,0:T(8,128)(2,1)}) %reduce-scatter.18.cloned.1.call-update) | async-done | bytes 720912 | tf_op jit(solution)/shard_map/reduce_scatter | solution.py:246
  1174.1 111.6 %reduce-scatter.20.cloned.1.call-done = bf16[1408,256]{1,0:T(8,128)(2,1)} async-done(((bf16[1408,2048]{1,0:T(8,128)(2,1)}), bf16[1408,256]{1,0:T(8,128)(2,1)}) %reduce-scatter.20.cloned.1.call-update) | async-done | bytes 720912 | tf_op jit(solution)/shard_map/reduce_scatter | solution.py:249
  (326 shorter events, 309.4 us)
Async XLA Ops:
  7.2 252.4 %copy-start = (bf16[512,2048]{1,0:T(8,128)(2,1)S(1)}, bf16[512,2048]{1,0:T(8,128)(2,1)}, u32[]{:S(2)}) copy-start(bf16[512,2048]{1,0:T(8,128)(2,1)} %param.29) | copy-start | bytes 6291460
  7.2 307.3 %all-reduce.8.cloned.1.call-start = ((), (), s32[]{:S(2)}) async-start(), calls=%async_computation.7 | async-start | bytes 4194304 | tf_op jit(solution)/shard_map/psum | solution.py:207
  18.8 53.5 %copy-start.15 = (f32[512,64]{0,1:T(8,128)}, f32[512,64]{0,1:T(8,128)S(1)}, u32[]{:S(2)}) copy-start(f32[512,64]{0,1:T(8,128)S(1)} %get-tuple-element.546) | copy-start | bytes 393220
  21.0 15.1 %collective-permute-start = (bf16[512,512]{0,1:T(8,128)(2,1)S(1)}, bf16[512,512]{0,1:T(8,128)(2,1)}, u32[]{:S(2)}, u32[]{:S(2)}) collective-permute-start(bf16[512,512]{0,1:T(8,128)(2,1)S(1)} %pad_maximum_fusion), channel_id=1, source_target_pairs={{0,4},{4,0},{8,12},{12,8},{16,20},{20,16},{24,28},{28,24},{1,5},{5... | collective-permute-start | bytes 1572872 | tf_op jit(solution)/shard_map/ppermute | solution.py:18
  37.9 24.5 %collective-permute-start.1 = (bf16[1024,512]{0,1:T(8,128)(2,1)S(1)}, bf16[1024,512]{0,1:T(8,128)(2,1)}, u32[]{:S(2)}, u32[]{:S(2)}) collective-permute-start(bf16[1024,512]{0,1:T(8,128)(2,1)S(1)} %maximum_select_fusion.2), channel_id=1, source_target_pairs={{0,8},{4,12},{8,0},{12,4},{16,24},{20,28},{24,16},{28,20},{1,9},{5... | collective-permute-start | bytes 3145736 | tf_op jit(solution)/shard_map/ppermute | solution.py:18
  66.1 92.1 %collective-permute-start.2 = (bf16[2048,512]{0,1:T(8,128)(2,1)}, bf16[2048,512]{0,1:T(8,128)(2,1)}, u32[]{:S(2)}, u32[]{:S(2)}) collective-permute-start(bf16[2048,512]{0,1:T(8,128)(2,1)} %maximum_select_fusion.1), channel_id=1, source_target_pairs={{0,16},{4,20},{8,24},{12,28},{16,0},{20,4},{24,8},{28,12},{1,17},{... | collective-permute-start | bytes 6291464 | tf_op jit(solution)/shard_map/ppermute | solution.py:18
  262.2 139.6 %all-reduce.10.cloned.1.call-start = ((), (), s32[]{:S(2)}) async-start(), calls=%async_computation.8 | async-start | bytes 4194304 | tf_op jit(solution)/shard_map/psum | solution.py:232
  318.0 8.1 slice-start.2
  326.2 14.2 %slice-start = ((s8[5767168]{0:T(1024)(128)(4,1)}), s8[4194304]{0:T(1024)(128)(4,1)S(1)}, s32[]{:S(2)}) async-start(s8[5767168]{0:T(1024)(128)(4,1)} %bitcast.260), calls=%async_computation.17 | async-start | bytes 8388608
  331.2 9.2 slice-start.1
  350.1 366.8 %reduce-scatter.14.cloned.1.call-start = ((), (), s32[]{:S(2)}) async-start(), calls=%async_computation.12 | async-start | bytes 2359296 | tf_op jit(solution)/shard_map/reduce_scatter | solution.py:342
  494.0 229.0 %reduce-scatter.8.cloned.1.call-start = ((), (), s32[]{:S(2)}) async-start(), calls=%async_computation.9 | async-start | bytes 2359296 | tf_op jit(solution)/shard_map/reduce_scatter | solution.py:333
  500.4 110.2 %collective-permute-start.3 = (bf16[2048,512]{1,0:T(8,128)(2,1)}, bf16[2048,512]{1,0:T(8,128)(2,1)}, u32[]{:S(2)}, u32[]{:S(2)}) collective-permute-start(bf16[2048,512]{1,0:T(8,128)(2,1)} %select_convert_fusion), channel_id=1, source_target_pairs={{0,16},{4,20},{8,24},{12,28},{16,0},{20,4},{24,8},{28,12},{1,17},{... | collective-permute-start | bytes 6291464 | tf_op jit(solution)/shard_map/ppermute | solution.py:18
  506.9 282.5 %reduce-scatter.10.cloned.1.call-start = ((), (), s32[]{:S(2)}) async-start(), calls=%async_computation.10 | async-start | bytes 1179648 | tf_op jit(solution)/shard_map/reduce_scatter | solution.py:336
  618.0 33.0 %collective-permute-start.4 = (bf16[1024,512]{1,0:T(8,128)(2,1)S(1)}, bf16[1024,512]{1,0:T(8,128)(2,1)}, u32[]{:S(2)}, u32[]{:S(2)}) collective-permute-start(bf16[1024,512]{1,0:T(8,128)(2,1)S(1)} %select_convert_fusion.1), channel_id=1, source_target_pairs={{0,8},{4,12},{8,0},{12,4},{16,24},{20,28},{24,16},{28,20},{1,9},{5... | collective-permute-start | bytes 3145736 | tf_op jit(solution)/shard_map/ppermute | solution.py:18
  654.2 15.2 %collective-permute-start.5 = (bf16[512,512]{1,0:T(8,128)(2,1)S(1)}, bf16[512,512]{1,0:T(8,128)(2,1)S(1)}, u32[]{:S(2)}, u32[]{:S(2)}) collective-permute-start(bf16[512,512]{1,0:T(8,128)(2,1)S(1)} %select_convert_fusion.2), channel_id=1, source_target_pairs={{0,4},{4,0},{8,12},{12,8},{16,20},{20,16},{24,28},{28,24},{1,5},{5... | collective-permute-start | bytes 1572872 | tf_op jit(solution)/shard_map/ppermute | solution.py:18
  675.7 180.3 %reduce-scatter.12.cloned.1.call-start = ((), (), s32[]{:S(2)}) async-start(), calls=%async_computation.11 | async-start | bytes 1179648 | tf_op jit(solution)/shard_map/reduce_scatter | solution.py:339
  677.7 265.9 %all-reduce.12.cloned.1.call-start = ((), (), s32[]{:S(2)}) async-start(), calls=%async_computation.16 | async-start | bytes 8388608 | tf_op jit(solution)/shard_map/psum | solution.py:220
  690.7 367.5 %reduce-scatter.16.cloned.1.call-start = ((), (), s32[]{:S(2)}) async-start(), calls=%async_computation.13 | async-start | bytes 6488064 | tf_op jit(solution)/shard_map/reduce_scatter | solution.py:243
  698.7 473.1 %reduce-scatter.18.cloned.1.call-start = ((), (), s32[]{:S(2)}) async-start(), calls=%async_computation.14 | async-start | bytes 6488064 | tf_op jit(solution)/shard_map/reduce_scatter | solution.py:246
  706.8 578.9 %reduce-scatter.20.cloned.1.call-start = ((), (), s32[]{:S(2)}) async-start(), calls=%async_computation.15 | async-start | bytes 6488064 | tf_op jit(solution)/shard_map/reduce_scatter | solution.py:249
  715.0 231.8 %copy-start.35 = (bf16[2048]{0:T(1024)(128)(2,1)S(1)}, bf16[2048]{0:T(1024)(128)(2,1)}, u32[]{:S(2)}) copy-start(bf16[2048]{0:T(1024)(128)(2,1)} %get-tuple-element.441) | copy-start | bytes 12292
  715.0 254.9 %copy-start.36 = (f32[512]{0:T(512)S(1)}, f32[512]{0:T(512)}, u32[]{:S(2)}) copy-start(f32[512]{0:T(512)} %get-tuple-element.547) | copy-start | bytes 6148
  969.9 318.1 %copy-start.1 = (bf16[512,2048]{1,0:T(8,128)(2,1)S(1)}, bf16[512,2048]{1,0:T(8,128)(2,1)}, u32[]{:S(2)}) copy-start(bf16[512,2048]{1,0:T(8,128)(2,1)} %param.29) | copy-start | bytes 6291460
  (41 other events, 174.1 us)
Sparse Core Ops, SparseCore 0:
  262.3 52.1 all-reduce.7
  350.2 51.4 all-reduce.9
  494.1 154.7 reduce-scatter.13
  652.3 70.6 reduce-scatter.7
  726.2 63.2 reduce-scatter.9
  792.7 63.2 reduce-scatter.11
  859.0 84.5 all-reduce.11
  947.3 110.8 reduce-scatter.15
  1061.8 109.9 reduce-scatter.17
  1175.3 110.3 reduce-scatter.19
where the time goes:
time: 1300 us
  waiting for transfers between devices  895 us (69%)
  matrix products  180 us (14%)
  other arithmetic  104 us (8%)
  local copies, waits for them, and re-layouts  56.9 us (4%)
  blocking collectives  22.5 us (2%)
  between operations  15.8 us (1%)
    ppermute x6, waiting for transfers between devices, swapped(): return lax.ppermute(value, axis, pairs)  267 us
    reduce_scatter x1, waiting for transfers between devices, shards(): lax.psum_scatter(grad_down.astype(jnp.bfloat16), 'wide', scatter_dimensio...  112 us
    reduce_scatter x1, waiting for transfers between devices, shards(): lax.psum_scatter(grad_up.astype(jnp.bfloat16), 'wide', scatter_dimension=...  111 us
    psum x1, waiting for transfers between devices, shards(): lax.psum(jnp.dot(inner_act, w_down, preferred_element_type=jnp.float32).a...  86 us
    reduce_scatter x1, waiting for transfers between devices, shards(): lax.psum_scatter(grad_gate.astype(jnp.bfloat16), 'wide', scatter_dimensio...  80.6 us
    reduce_scatter x1, waiting for transfers between devices, shards(): lax.psum_scatter(grad_value.astype(jnp.bfloat16), 'wide', scatter_dimensi...  64.9 us
    reduce_scatter x1, waiting for transfers between devices, shards(): lax.psum_scatter(grad_key.astype(jnp.bfloat16), 'wide', scatter_dimension...  64.7 us
    psum x1, waiting for transfers between devices, shards(): lax.psum(jnp.dot(mixed_heads, w_out, preferred_element_type=jnp.float32)....  52.2 us
  transfers between devices with their start and end apart: 16, of which 15 were waited for; matrix products, arithmetic and copies ran while one was open for 7% of the time, Pallas kernels for 0%

commit v1 on v0

v1 whole, which is shorter than its diff:
```python
import functools

import jax
import jax.numpy as jnp
from jax import lax
from jax.experimental import pallas as pl
from jax.experimental.pallas import tpu as pltpu
from jax.sharding import PartitionSpec as P

HD = 128
EPSILON = 1e-05
NEGATIVE = -1e30
BASE = 10000.0
LOG2E = 1.4426950408889634
SCORE = HD ** (-0.5) * LOG2E
FACTOR = HD ** (-0.5)
BF = jnp.bfloat16
F32 = jnp.float32
NT = (((1,), (1,)), ((), ()))
TN = (((0,), (0,)), ((), ()))
VM = pl.BlockSpec(memory_space=pltpu.VMEM)
SM = pl.BlockSpec(memory_space=pltpu.SMEM)
ANY = pl.BlockSpec(memory_space=pl.ANY)


def dot(a, b, dims=(((1,), (0,)), ((), ()))):
    return lax.dot_general(a, b, dims, preferred_element_type=F32)


def narrow_swap(value, mask):
    pairs = [(n, n ^ mask) for n in range(lax.axis_size("narrow"))]
    return lax.ppermute(value, "narrow", pairs)


def wide_swap(value):
    return lax.ppermute(value, "wide", [(w, w ^ 1) for w in range(lax.axis_size("wide"))])


def wide_ring(value, group):
    ring = group // 2
    pairs = []
    for w in range(lax.axis_size("wide")):
        base, member = w // group * group, w % group
        pairs.append((w, base + (member // 2 + 1) % ring * 2 + member % 2))
    return lax.ppermute(value, "wide", pairs)


def rope(value, cosine, sine):
    return value * cosine + pltpu.roll(value, HD // 2, 1) * sine


def norm_kv_kernel(core, x_ref, gain_ref, wk_ref, wv_ref, cos_ref, sin_ref, normed_ref, kv_ref):
    x = x_ref[...].astype(F32)
    scale = lax.rsqrt(jnp.mean(x * x, axis=1, keepdims=True) + EPSILON)
    normed = (x * scale * gain_ref[...].astype(F32)).astype(BF)
    normed_ref[...] = normed
    width = wk_ref.shape[1]
    keys = dot(normed, wk_ref[...])
    for h in range(width // HD):
        cols = slice(h * HD, (h + 1) * HD)
        kv_ref[:, cols] = rope(keys[:, cols], cos_ref[...], sin_ref[...]).astype(BF)
    kv_ref[:, width:] = dot(normed, wv_ref[...]).astype(BF)


def norm_kv(core, tokens, gain, wk, wv, cosine, sine):
    rows, width = tokens.shape
    half = rows // 2
    full = lambda w: pl.BlockSpec(w.shape, lambda i, c: (0, 0))
    return pl.pallas_call(
        norm_kv_kernel,
        out_shape=(
            jax.ShapeDtypeStruct((rows, width), BF),
            jax.ShapeDtypeStruct((rows, 2 * wk.shape[1]), BF),
        ),
        grid_spec=pltpu.PrefetchScalarGridSpec(
            num_scalar_prefetch=1,
            grid=(2,),
            in_specs=[
                pl.BlockSpec((half, width), lambda i, c: (i ^ c[0], 0)),
                full(gain),
                full(wk),
                full(wv),
                pl.BlockSpec((half, HD), lambda i, c: (i, 0)),
                pl.BlockSpec((half, HD), lambda i, c: (i, 0)),
            ],
            out_specs=[
                pl.BlockSpec((half, width), lambda i, c: (i, 0)),
                pl.BlockSpec((half, 2 * wk.shape[1]), lambda i, c: (i, 0)),
            ],
        ),
        name="norm_kv",
    )(core, tokens, gain, wk, wv, cosine, sine)


def query_kernel(x_ref, w_ref, cos_ref, sin_ref, out_ref):
    raw = dot(x_ref[...], w_ref[...])
    for h in range(raw.shape[1] // HD):
        cols = slice(h * HD, (h + 1) * HD)
        out_ref[:, cols] = rope(raw[:, cols], cos_ref[...], sin_ref[...]).astype(BF)


def query_proj(x, w, cosine, sine):
    rows, width = x.shape
    half = rows // 2
    return pl.pallas_call(
        query_kernel,
        out_shape=jax.ShapeDtypeStruct((rows, w.shape[1]), BF),
        grid=(2,),
        in_specs=[
            pl.BlockSpec((half, width), lambda i: (i, 0)),
            pl.BlockSpec(w.shape, lambda i: (0, 0)),
            pl.BlockSpec((half, HD), lambda i: (i, 0)),
            pl.BlockSpec((half, HD), lambda i: (i, 0)),
        ],
        out_specs=pl.BlockSpec((half, w.shape[1]), lambda i: (i, 0)),
        cost_estimate=pl.CostEstimate(
            flops=2 * rows * width * w.shape[1], bytes_accessed=6 << 20, transcendentals=0
        ),
        name="query_proj",
    )(x, w, cosine, sine)


def fetch_slots(slot_refs, kv_ref, sems):
    rows = slot_refs[0].shape[0]
    copies = [
        pltpu.make_async_copy(ref, kv_ref.at[pl.ds(j * rows, rows), :], sems.at[j])
        for j, ref in enumerate(slot_refs)
    ]
    for copy in copies:
        copy.start()
    for copy in copies:
        copy.wait()


def allowed(pk, size, span, pos, low):
    key_pos = pk * size + lax.broadcasted_iota(jnp.int32, (size, span), 0)
    return (key_pos <= pos) & (key_pos >= low)


def attn_fwd_kernel(slots, *refs):
    meta, q_ref, pos_ref, low_ref = refs[:4]
    slot_refs = refs[4 : 4 + slots]
    mixed_ref, lse_ref, kv_ref, acc_ref, sems = refs[4 + slots :]
    fetch_slots(slot_refs, kv_ref, sems)
    size = q_ref.shape[0] // 2
    kv_width = kv_ref.shape[1] // 2
    groups = kv_width // HD
    for i in range(2):
        rows = slice(i * size, (i + 1) * size)
        pos = jnp.tile(pos_ref[0:1, rows], (1, 2))
        low = jnp.tile(low_ref[0:1, rows], (1, 2))
        for g in range(groups):
            queries = [
                q_ref[rows, (2 * g + r) * HD : (2 * g + r + 1) * HD] for r in range(2)
            ]
            acc_ref[...] = jnp.zeros_like(acc_ref)

            def body(pk, carry):
                peak, total = carry
                spot = pl.multiple_of(meta[4 + pk] * size, size)
                keys = kv_ref[pl.ds(spot, size), g * HD : (g + 1) * HD]
                values = kv_ref[pl.ds(spot, size), kv_width + g * HD : kv_width + (g + 1) * HD]
                scores = jnp.concatenate([dot(keys, q, NT) for q in queries], axis=1) * SCORE
                scores = jnp.where(allowed(pk, size, 2 * size, pos, low), scores, NEGATIVE)
                peak_new = jnp.maximum(peak, jnp.max(scores, axis=0, keepdims=True))
                alpha = jnp.exp2(peak - peak_new)
                probs = jnp.exp2(scores - peak_new)
                total = total * alpha + jnp.sum(probs, axis=0, keepdims=True)
                acc_ref[...] = acc_ref[...] * alpha + dot(values, probs.astype(BF), TN)
                return peak_new, total

            start = (jnp.full((1, 2 * size), NEGATIVE, F32), jnp.zeros((1, 2 * size), F32))
            peak, total = lax.fori_loop(meta[i], meta[2 + i] + 1, body, start)
            lse_ref[pl.ds(i * groups + g, 1), :] = peak + jnp.log2(total)
            out = acc_ref[...] * (1.0 / total)
            for r in range(2):
                mixed_ref[rows, (2 * g + r) * HD : (2 * g + r + 1) * HD] = (
                    out[:, r * size : (r + 1) * size].T.astype(BF)
                )


def attn_fwd(meta, q, pos, low, slots):
    rows, q_width = q.shape
    kv_width = slots[0].shape[1]
    return pl.pallas_call(
        functools.partial(attn_fwd_kernel, len(slots)),
        out_shape=(
            jax.ShapeDtypeStruct((rows, q_width), BF),
            jax.ShapeDtypeStruct((q_width // HD, rows), F32),
        ),
        in_specs=[SM, VM, VM, VM] + [ANY] * len(slots),
        out_specs=[VM, VM],
        scratch_shapes=[
            pltpu.VMEM((len(slots) * rows, kv_width), BF),
            pltpu.VMEM((HD, rows), F32),
            pltpu.SemaphoreType.DMA((len(slots),)),
        ],
        name="attn_fwd",
    )(meta, q, pos, low, *slots)


def attn_bwd_kernel(slots, *refs):
    meta, q_ref, pos_ref, low_ref, lse_ref, mixed_ref, dmix_ref, cos_ref, sin_ref = refs[:9]
    slot_refs = refs[9 : 9 + slots]
    dq_ref = refs[9 + slots]
    dkv_refs = refs[10 + slots : 10 + 2 * slots]
    kv_ref, dkv_ref, dq_acc, sems = refs[10 + 2 * slots :]
    fetch_slots(slot_refs, kv_ref, sems)
    dkv_ref[...] = jnp.zeros_like(dkv_ref)
    rows_all = q_ref.shape[0]
    size = rows_all // 2
    kv_width = kv_ref.shape[1] // 2
    groups = kv_width // HD
    for i in range(2):
        rows = slice(i * size, (i + 1) * size)
        pos = jnp.tile(pos_ref[0:1, rows], (1, 2))
        low = jnp.tile(low_ref[0:1, rows], (1, 2))
        for g in range(groups):
            cols = [slice((2 * g + r) * HD, (2 * g + r + 1) * HD) for r in range(2)]
            queries = jnp.concatenate([q_ref[rows, c] for c in cols], axis=0)
            grads = jnp.concatenate([dmix_ref[rows, c] for c in cols], axis=0)
            outs = jnp.concatenate([mixed_ref[rows, c] for c in cols], axis=0)
            delta = jnp.sum((grads.astype(F32) * outs.astype(F32)).T, axis=0, keepdims=True)
            lse = lse_ref[pl.ds(i * groups + g, 1), :]
            dq_acc[...] = jnp.zeros_like(dq_acc)

            def body(pk, carry):
                spot = pl.multiple_of(meta[4 + pk] * size, size)
                key_cols = slice(g * HD, (g + 1) * HD)
                value_cols = slice(kv_width + g * HD, kv_width + (g + 1) * HD)
                keys = kv_ref[pl.ds(spot, size), key_cols]
                values = kv_ref[pl.ds(spot, size), value_cols]
                scores = dot(keys, queries, NT) * SCORE
                probs = jnp.where(
                    allowed(pk, size, 2 * size, pos, low), jnp.exp2(scores - lse), 0.0
                )
                d_probs = dot(values, grads, NT)
                d_scores = (probs * (d_probs - delta)).astype(BF)
                dkv_ref[pl.ds(spot, size), value_cols] += dot(probs.astype(BF), grads)
                dkv_ref[pl.ds(spot, size), key_cols] += dot(d_scores, queries) * FACTOR
                dq_acc[...] += dot(d_scores, keys, TN)
                return carry

            lax.fori_loop(meta[i], meta[2 + i] + 1, body, 0)
            for r in range(2):
                part = dq_acc[r * size : (r + 1) * size, :] * FACTOR
                dq_ref[rows, cols[r]] = rope(part, cos_ref[rows, :], -sin_ref[rows, :]).astype(BF)
    for j, ref in enumerate(dkv_refs):
        ref[...] = dkv_ref[j * rows_all : (j + 1) * rows_all, :].astype(BF)


def attn_bwd(meta, q, pos, low, lse, mixed, dmix, cosine, sine, slots):
    rows, q_width = q.shape
    kv_width = slots[0].shape[1]
    count = len(slots)
    outs = pl.pallas_call(
        functools.partial(attn_bwd_kernel, count),
        out_shape=[jax.ShapeDtypeStruct((rows, q_width), BF)]
        + [jax.ShapeDtypeStruct((rows, kv_width), BF)] * count,
        in_specs=[SM] + [VM] * 8 + [ANY] * count,
        out_specs=[VM] * (1 + count),
        scratch_shapes=[
            pltpu.VMEM((count * rows, kv_width), BF),
            pltpu.VMEM((count * rows, kv_width), F32),
            pltpu.VMEM((rows, HD), F32),
            pltpu.SemaphoreType.DMA((count,)),
        ],
        name="attn_bwd",
    )(meta, q, pos, low, lse, mixed, dmix, cosine, sine, *slots)
    return outs[0], outs[1:]


def norm_backward(source, scale_rows, gain, upstream):
    weighted = upstream * gain
    average = jnp.mean(weighted * source, axis=1, keepdims=True)
    return scale_rows * weighted - source * scale_rows**3 * average


def shards(
    tokens,
    cotangent,
    keep_mask,
    doc_lengths,
    block_order,
    gain_attn,
    w_query,
    w_key,
    w_value,
    w_out,
    gain_dense,
    w_gate,
    w_up,
    w_down,
):
    rows, width = tokens.shape
    half = rows // 2
    wide = lax.axis_size("wide")
    group = wide // block_order.shape[0]
    ring = group // 2
    wide_index = lax.axis_index("wide")
    member = wide_index % group
    seq_index = wide_index // group
    side = wide_index % 2
    core = lax.axis_index("narrow") % 2
    strip = width // wide
    turns = wide // 2

    def ordered(mine, other):
        return jnp.where(
            core == 0,
            jnp.concatenate([mine, other], axis=0),
            jnp.concatenate([other, mine], axis=0),
        )

    def own_half(value):
        return lax.dynamic_slice_in_dim(value, core * half, half)

    def other_half(value):
        return lax.dynamic_slice_in_dim(value, (1 - core) * half, half)

    order_row = lax.dynamic_index_in_dim(block_order, seq_index, 0, keepdims=False)
    length_row = lax.dynamic_index_in_dim(doc_lengths, seq_index, 0, keepdims=False)
    doc_ends = jnp.cumsum(length_row)
    places = jnp.stack([member * 2 + core, member * 2 + 1 - core])
    chosen = jnp.sum(
        jnp.where(places[:, None] == jnp.arange(2 * group)[None, :], order_row[None, :], 0), axis=1
    )
    pos = (chosen[:, None] * half + jnp.arange(half, dtype=jnp.int32)[None, :]).reshape(-1)
    low = jnp.max(jnp.where(doc_ends[None, :] <= pos[:, None], doc_ends[None, :], 0), axis=1)
    block_low = low.reshape(2, half)[:, 0] // half
    stored = jnp.sum(
        jnp.where(
            order_row[None, :] == jnp.arange(2 * group)[:, None], jnp.arange(2 * group)[None, :], 0
        ),
        axis=1,
    )
    owner = stored // 2
    slot = (member // 2 - owner // 2) % ring + ring * (owner % 2 != side).astype(jnp.int32)
    spots = slot * 2 + (stored % 2 != core).astype(jnp.int32)
    meta = jnp.concatenate([block_low, chosen, spots]).astype(jnp.int32)
    frequency = BASE ** (-(jnp.arange(HD // 2, dtype=F32) * 2.0) / HD)
    angles = pos.astype(F32)[:, None] * frequency[None, :]
    cosine = jnp.cos(angles)
    sine = jnp.sin(angles)
    cosine = jnp.concatenate([cosine, cosine], axis=1)
    sine = jnp.concatenate([-sine, sine], axis=1)
    pos_row = pos[None, :]
    low_row = low[None, :]

    core_arr = core.astype(jnp.int32)[None]
    normed_one, both = norm_kv(core_arr, tokens, gain_attn[None, :], w_key, w_value, cosine, sine)
    near = [both]
    far = [wide_swap(both)]
    for step in range(1, ring):
        near.append(wide_ring(near[-1], group))
        far.append(wide_swap(near[-1]))
    slots = near + far
    query = query_proj(normed_one, w_query, cosine, sine)
    mixed, lse = attn_fwd(meta, query, pos_row, low_row, slots)

    def reduce_narrow(other_part, own_part):
        got = narrow_swap(other_part, 1)
        held = (own_part + got.astype(F32)).astype(BF)
        return held.astype(F32) + narrow_swap(held, 2).astype(F32)

    def cut(value):
        return value[:half], value[half:]

    mixed_own, mixed_other = cut(mixed)
    attn_out = reduce_narrow(dot(mixed_other, w_out).astype(BF), dot(mixed_own, w_out))
    source = own_half(tokens).astype(F32)
    keep_own = own_half(keep_mask).astype(F32)[:, None]
    hidden_one = source + keep_own * attn_out
    gain_two = gain_dense.astype(F32)
    scale_two = lax.rsqrt(jnp.mean(hidden_one * hidden_one, axis=1, keepdims=True) + EPSILON)
    normed_two_own = (hidden_one * scale_two * gain_two).astype(BF)
    normed_two = jnp.concatenate([normed_two_own, narrow_swap(normed_two_own, 1)], axis=0)

    keep_rel = jnp.concatenate([own_half(keep_mask), other_half(keep_mask)])[:, None]
    cot_rel = jnp.concatenate([own_half(cotangent), other_half(cotangent)])
    d_dense = jnp.where(keep_rel > 0, cot_rel, jnp.zeros_like(cot_rel))
    d_inner = dot(d_dense, w_down, NT)
    gate = dot(normed_two, w_gate)
    up = dot(normed_two, w_up)
    sigma = jax.nn.sigmoid(gate)
    silu = gate * sigma
    inner = (silu * up).astype(BF)
    d_gate = (d_inner * up * sigma * (1.0 + gate * (1.0 - sigma))).astype(BF)
    d_up = (d_inner * silu).astype(BF)

    dg_own, dg_other = cut(d_gate)
    du_own, du_other = cut(d_up)

    def back_dense(dg, du):
        return dot(dg, w_gate, NT) + dot(du, w_up, NT)

    d_normed_two = reduce_narrow(back_dense(dg_other, du_other).astype(BF), back_dense(dg_own, du_own))
    inner_own, inner_other = cut(inner)
    dense_out = reduce_narrow(dot(inner_other, w_down).astype(BF), dot(inner_own, w_down))
    output_own = (hidden_one + keep_own * dense_out).astype(BF)
    output = ordered(output_own, narrow_swap(output_own, 1))

    upstream = own_half(cotangent).astype(F32)
    d_hidden = upstream + norm_backward(hidden_one, scale_two, gain_two, d_normed_two)
    d_attn_own = (keep_own * d_hidden).astype(BF)
    d_attn = jnp.concatenate([d_attn_own, narrow_swap(d_attn_own, 1)], axis=0)

    def strips(value):
        cells = value.reshape(value.shape[0], turns, 2, strip)
        mine = lax.dynamic_index_in_dim(cells, side, 2, keepdims=False)
        theirs = lax.dynamic_index_in_dim(cells, 1 - side, 2, keepdims=False)
        flat = (value.shape[0], turns * strip)
        return jnp.concatenate([mine.reshape(flat), wide_swap(theirs.reshape(flat))], axis=0)

    def paired(value):
        return jnp.concatenate([value, wide_swap(value)], axis=0)

    def ring_sum(part):
        carried = None
        for step in range(1, turns + 1):
            piece = part((wide_index // 2 - step) % turns)
            if carried is not None:
                piece = piece + carried.astype(F32)
            if step == turns:
                return piece
            carried = wide_ring(piece.astype(BF), wide)

    def strip_of(value, turn):
        return lax.dynamic_slice_in_dim(value, turn * strip, strip, axis=1)

    d_dense_strips = strips(d_dense)
    normed_two_strips = strips(normed_two)
    normed_one_strips = strips(normed_one)
    d_attn_strips = strips(d_attn)
    inner_two = paired(inner)
    d_gate_two = paired(d_gate)
    d_up_two = paired(d_up)
    grad_down = ring_sum(lambda t: dot(inner_two, strip_of(d_dense_strips, t), TN))
    grad_gate = ring_sum(lambda t: dot(strip_of(normed_two_strips, t), d_gate_two, TN))
    grad_up = ring_sum(lambda t: dot(strip_of(normed_two_strips, t), d_up_two, TN))

    d_mixed = dot(d_attn, w_out, NT).astype(BF)
    d_query, d_slots = attn_bwd(
        meta, query, pos_row, low_row, lse, mixed, d_mixed, cosine, sine, slots
    )
    mixed_two = paired(mixed)
    grad_out = ring_sum(lambda t: dot(mixed_two, strip_of(d_attn_strips, t), TN))

    carried = None
    for step in [*range(1, ring), 0]:
        piece = d_slots[step].astype(F32) + wide_swap(d_slots[ring + step]).astype(F32)
        if carried is not None:
            piece = piece + carried.astype(F32)
        if step:
            carried = wide_ring(piece.astype(BF), group)
    kv_width = w_key.shape[1]
    d_keys = piece[:, :kv_width].reshape(rows, kv_width // HD, HD)
    turned = jnp.concatenate([d_keys[..., HD // 2 :], d_keys[..., : HD // 2]], axis=-1)
    d_keys = d_keys * cosine[:, None, :] - turned * sine[:, None, :]
    d_kv = jnp.concatenate([d_keys.reshape(rows, kv_width), piece[:, kv_width:]], axis=1).astype(BF)
    d_key, d_value = d_kv[:, :kv_width], d_kv[:, kv_width:]

    def back_attn(part):
        return (
            dot(part(d_query), w_query, NT)
            + dot(part(d_key), w_key, NT)
            + dot(part(d_value), w_value, NT)
        )

    d_normed_one = reduce_narrow(
        back_attn(lambda v: v[half:]).astype(BF), back_attn(lambda v: v[:half])
    )
    gain_one = gain_attn.astype(F32)
    scale_one = lax.rsqrt(jnp.mean(source * source, axis=1, keepdims=True) + EPSILON)
    grad_own = (d_hidden + norm_backward(source, scale_one, gain_one, d_normed_one)).astype(BF)
    grad_tokens = ordered(grad_own, narrow_swap(grad_own, 1))

    d_query_two = paired(d_query)
    d_kv_two = paired(d_kv)
    grad_query = ring_sum(lambda t: dot(strip_of(normed_one_strips, t), d_query_two, TN))
    grad_kv = ring_sum(lambda t: dot(strip_of(normed_one_strips, t), d_kv_two, TN))
    grad_key, grad_value = grad_kv[:, :kv_width], grad_kv[:, kv_width:]

    def strip_rows(weight):
        return lax.dynamic_slice_in_dim(weight, wide_index * strip, strip).astype(F32)

    def gain_grad(pairs, gain):
        local = sum(jnp.sum(strip_rows(w) * g, axis=1) for w, g in pairs)[None, :]
        local = local + narrow_swap(local, 1)
        local = local + narrow_swap(local, 2)
        return local[0] / lax.dynamic_slice_in_dim(gain, wide_index * strip, strip)

    grad_gain_two = gain_grad([(w_gate, grad_gate), (w_up, grad_up)], gain_two)
    grad_gain_one = gain_grad(
        [(w_query, grad_query), (w_key, grad_key), (w_value, grad_value)], gain_one
    )
    return (
        output,
        grad_tokens,
        grad_gain_one,
        grad_query,
        grad_key,
        grad_value,
        grad_out,
        grad_gain_two,
        grad_gate,
        grad_up,
        grad_down,
    )


def solution(mesh):
    placed = (
        P("wide", None),
        P("wide", None),
        P("wide"),
        P(),
        P(),
        P(),
        P(None, "narrow"),
        P(None, "narrow"),
        P(None, "narrow"),
        P("narrow", None),
        P(),
        P(None, "narrow"),
        P(None, "narrow"),
        P("narrow", None),
    )
    return jax.shard_map(
        shards,
        mesh=mesh,
        in_specs=placed,
        out_specs=(
            P("wide", None),
            P("wide", None),
            P("wide"),
            P("wide", "narrow"),
            P("wide", "narrow"),
            P("wide", "narrow"),
            P("narrow", "wide"),
            P("wide"),
            P("wide", "narrow"),
            P("wide", "narrow"),
            P("narrow", "wide"),
        ),
        check_vma=False,
    )
```

time: 1300 us -> 617 us (0.47)
  waiting for transfers between devices: 895 us -> 277 us
  matrix products: 180 us -> 107 us
  other arithmetic: 104 us -> 32.1 us
  starting transfers between devices: 12.6 us -> 59.3 us
  Pallas kernels: 0 us -> 39.3 us
  local copies, waits for them, and re-layouts: 56.9 us -> 92.6 us
  blocking collectives: 22.5 us -> 0 us
  between operations: 15.8 us -> 1.98 us
    reduce_scatter x7 -> x0, waiting for transfers between devices: 437 us -> none  [the longest x1 112 us: shards(): lax.psum_scatter(grad_down.astype(jnp.bfloat16), 'wide', scatter_dimensio...]
    psum x3 -> x0, waiting for transfers between devices: 190 us -> none  [the longest x1 86 us: shards(): lax.psum(jnp.dot(inner_act, w_down, preferred_element_type=jnp.float32).a...]
    dot_general x49 -> x42, matrix products: 180 us -> 107 us  [dot(): return lax.dot_general(a, b, dims, preferred_element_type=F32)]
    ppermute x6 -> x58, starting transfers between devices: 11.5 us -> 59.3 us  [the longest x24 28.9 us: wide_ring(): return lax.ppermute(value, 'wide', pairs)]
    pallas_call x0 -> x4, Pallas kernels: none -> 39.3 us  [the longest x1 17.5 us: attn_bwd(): pl.pallas_call(functools.partial(attn_bwd_kernel, count), out_shape=[jax....]
    unnamed x94 -> x144, local copies, waits for them, and re-layouts: 8.75 us -> 43 us
    reduce_sum x9 -> x6, other arithmetic: 31.7 us -> 5.67 us  [the longest x1 2.49 us: shards(): jnp.mean(hidden_one * hidden_one, axis=1, keepdims=True) + EPSILON]
    unnamed x1 -> x0, blocking collectives: 22.5 us -> none
  transfers between devices with their start and end apart: 16 -> 58, of which waited for: 15 -> 27; matrix products, arithmetic and copies ran while one was open for 7% -> 35% of each run, Pallas kernels for 0% -> 4%
where the time goes in v1:
time: 617 us; the launch traced here: 609 us
  waiting for transfers between devices  277 us (45%)
  matrix products  107 us (17%)
  local copies, waits for them, and re-layouts  92.6 us (15%)
  starting transfers between devices  59.3 us (10%)
  Pallas kernels  39.3 us (6%)
  other arithmetic  32.1 us (5%)
    ppermute x24, waiting for transfers between devices, wide_ring(): return lax.ppermute(value, 'wide', pairs)  135 us
    ppermute x18, waiting for transfers between devices, wide_swap(): lax.ppermute(value, 'wide', [(w, w ^ 1) for w in range(lax.axis_size('wid...  130 us
    dot_general x42, matrix products, dot(): return lax.dot_general(a, b, dims, preferred_element_type=F32)  107 us
    unnamed x144, local copies, waits for them, and re-layouts  43 us
    ppermute x24, starting transfers between devices, wide_ring(): return lax.ppermute(value, 'wide', pairs)  28.9 us
    dynamic_slice x4, local copies, waits for them, and re-layouts, strips(): theirs = lax.dynamic_index_in_dim(cells, 1 - side, 2, keepdims=False)  22.7 us
    ppermute x18, starting transfers between devices, wide_swap(): lax.ppermute(value, 'wide', [(w, w ^ 1) for w in range(lax.axis_size('wid...  21.4 us
    pallas_call x1, Pallas kernels, attn_bwd(): pl.pallas_call(functools.partial(attn_bwd_kernel, count), out_shape=[jax....  17.5 us
  transfers between devices with their start and end apart: 58, of which 27 were waited for; matrix products, arithmetic and copies ran while one was open for 35% of the time, Pallas kernels for 4%

profile of v1, /device:TPU:0, one launch (start us, length us, event | category | flops | bytes accessed | tf_op | source)
XLA Modules:
  0.0 609.4 jit_solution(7717083899563314418)
XLA Ops:
  13.0 14.2 %collective-permute-done.refs_5_.refs_10_ = bf16[512,512]{1,0:T(8,128)(2,1)S(1)} collective-permute-done((bf16[512,512]{1,0:T(8,128)(2,1)}, bf16[512,512]{1,0:T(8,128)(2,1)S(1)}, u32[]{:S(2)}, u32[]{:S(2)}) %collective-permute-start) | collective-permute-done | bytes 524320 | tf_op jit(solution)/shard_map/ppermute | solution.py:45
  27.2 14.9 %collective-permute-done.1.refs_6_.refs_11_ = bf16[512,512]{1,0:T(8,128)(2,1)S(1)} collective-permute-done((bf16[512,512]{1,0:T(8,128)(2,1)S(1)}, bf16[512,512]{1,0:T(8,128)(2,1)S(1)}, u32[]{:S(2)}, u32[]{:S(2)}) %collective-permute-start.1) | collective-permute-done | bytes 524320 | tf_op jit(solution)/shard_map/ppermute | solution.py:45
  57.9 10.4 %collective-permute-done.4.refs_9_.refs_14_ = bf16[512,512]{1,0:T(8,128)(2,1)S(1)} collective-permute-done((bf16[512,512]{1,0:T(8,128)(2,1)S(1)}, bf16[512,512]{1,0:T(8,128)(2,1)S(1)}, u32[]{:S(2)}, u32[]{:S(2)}) %collective-permute-start.4) | collective-permute-done | bytes 524320 | tf_op jit(solution)/shard_map/ppermute | solution.py:36
  68.3 11.2 %collective-permute-done.5.refs_10_.refs_15_ = bf16[512,512]{1,0:T(8,128)(2,1)S(1)} collective-permute-done((bf16[512,512]{1,0:T(8,128)(2,1)S(1)}, bf16[512,512]{1,0:T(8,128)(2,1)S(1)}, u32[]{:S(2)}, u32[]{:S(2)}) %collective-permute-start.5) | collective-permute-done | bytes 524320 | tf_op jit(solution)/shard_map/ppermute | solution.py:36
  79.6 8.7 %collective-permute-done.6.refs_11_.refs_16_ = bf16[512,512]{1,0:T(8,128)(2,1)S(1)} collective-permute-done((bf16[512,512]{1,0:T(8,128)(2,1)}, bf16[512,512]{1,0:T(8,128)(2,1)S(1)}, u32[]{:S(2)}, u32[]{:S(2)}) %collective-permute-start.6) | collective-permute-done | bytes 524320 | tf_op jit(solution)/shard_map/ppermute | solution.py:36
  89.1 12.4 %attn_fwd.1 = (bf16[512,512]{1,0:T(8,128)(2,1)}, f32[4,512]{1,0:T(4,128)}) custom-call(s32[20]{0:T(128)} %pad_add_fusion.1.refs_0_, bf16[512,512]{1,0:T(8,128)(2,1)} %query_proj.1.refs_1_, s32[1,512]{1,0:T(1,128)} %bitcast.95, s32[1,512]{1,0:T(1,128)} %bitcast.93, bf16[512,512]{1,0:T(8,128)(2,1)} %get-tuple-element.25.refs_4_.refs_9_, ...), custom_call_target="tpu_custom_call" | custom-call | tf_op jit(solution)/shard_map/attn_fwd/pallas_call | solution.py:185
  125.6 7.6 %collective-permute-done.8 = bf16[256,2048]{1,0:T(8,128)(2,1)} collective-permute-done((bf16[256,2048]{1,0:T(8,128)(2,1)}, bf16[256,2048]{1,0:T(8,128)(2,1)}, u32[]{:S(2)}, u32[]{:S(2)}) %collective-permute-start.8) | collective-permute-done | bytes 1048608 | tf_op jit(solution)/shard_map/ppermute | solution.py:32
  164.5 6.7 %collective-permute-done.37 = bf16[512,512]{1,0:T(8,128)(2,1)S(1)} collective-permute-done((bf16[512,512]{1,0:T(8,128)(2,1)}, bf16[512,512]{1,0:T(8,128)(2,1)S(1)}, u32[]{:S(2)}, u32[]{:S(2)}) %collective-permute-start.37) | collective-permute-done | bytes 524320 | tf_op jit(solution)/shard_map/ppermute | solution.py:36
  171.2 6.7 %fusion.122 = f32[512,1408]{1,0:T(8,128)S(1)} fusion(bf16[2048,1408]{1,0:T(8,128)(2,1)} %param.26, bf16[256,2048]{1,0:T(8,128)(2,1)} %collective-permute-done.9, bf16[256,2048]{1,0:T(8,128)(2,1)} %multiply_convert_fusion.4), kind=kOutput, calls=%fused_computation.256 | convolution fusion | flops 2956984320 | bytes 10747904 | tf_op jit(solution)/shard_map/dot_general | solution.py:27
  178.0 7.9 %multiply_convert_fusion = (bf16[512,1408]{1,0:T(8,128)(2,1)}, bf16[512,1408]{1,0:T(8,128)(2,1)S(1)}, bf16[512,1408]{1,0:T(8,128)(2,1)}) fusion(f32[512,1408]{1,0:T(8,128)S(1)} %fusion.20, f32[512,1408]{1,0:T(8,128)S(1)} %fusion.122, bf16[2048,1408]{1,0:T(8,128)(2,1)S(1)} %bitcast.113, bf16[256,2048]{1,0:T(8,128)(2,1)} %collective-permute-done.9, ...), kind=kOutput, calls=%fused_computation.39 | convolution fusion | flops 2967797760 | bytes 17956864 | tf_op jit(solution)/shard_map/dot_general | solution.py:27
  212.5 6.3 %constant_dynamic-slice_fusion.2 = (bf16[512,4,1,256]{3,2,1,0:T(2,128)(2,1)}, bf16[512,4,1,256]{3,2,1,0:T(2,128)(2,1)}) fusion(bf16[512,4,2,256]{3,2,1,0:T(2,128)(2,1)S(1)} %copy-done.11, s32[]{:T(128)S(6)} %select_n.249, s32[]{:T(128)S(6)} %select_n.248), kind=kLoop, calls=%fused_computation.186 | loop fusion | bytes 4194312 | tf_op jit(solution)/shard_map/jit(dynamic_index_in_dim)/dynamic_slice | solution.py:411
  247.8 57.0 %collective-permute-done.42 = bf16[512,1024]{0,1:T(8,128)(2,1)S(1)} collective-permute-done((bf16[512,1024]{0,1:T(8,128)(2,1)}, bf16[512,1024]{0,1:T(8,128)(2,1)S(1)}, u32[]{:S(2)}, u32[]{:S(2)}) %collective-permute-start.42) | collective-permute-done | bytes 1048608 | tf_op jit(solution)/shard_map/ppermute | solution.py:36
  314.8 12.3 %collective-permute-done.55 = bf16[1408,256]{1,0:T(8,128)(2,1)S(1)} collective-permute-done((bf16[1408,256]{1,0:T(8,128)(2,1)S(1)}, bf16[1408,256]{1,0:T(8,128)(2,1)S(1)}, u32[]{:S(2)}, u32[]{:S(2)}) %collective-permute-start.55) | collective-permute-done | bytes 720928 | tf_op jit(solution)/shard_map/ppermute | solution.py:45
  329.9 12.6 %collective-permute-done.48 = bf16[256,1408]{1,0:T(8,128)(2,1)S(1)} collective-permute-done((bf16[256,1408]{1,0:T(8,128)(2,1)S(1)}, bf16[256,1408]{1,0:T(8,128)(2,1)S(1)}, u32[]{:S(2)}, u32[]{:S(2)}) %collective-permute-start.48) | collective-permute-done | bytes 720928 | tf_op jit(solution)/shard_map/ppermute | solution.py:45
  345.4 12.6 %collective-permute-done.44 = bf16[256,1408]{1,0:T(8,128)(2,1)S(1)} collective-permute-done((bf16[256,1408]{1,0:T(8,128)(2,1)S(1)}, bf16[256,1408]{1,0:T(8,128)(2,1)S(1)}, u32[]{:S(2)}, u32[]{:S(2)}) %collective-permute-start.44) | collective-permute-done | bytes 720928 | tf_op jit(solution)/shard_map/ppermute | solution.py:45
  361.9 26.9 %collective-permute-done.49 = bf16[256,1408]{1,0:T(8,128)(2,1)S(1)} collective-permute-done((bf16[256,1408]{1,0:T(8,128)(2,1)S(1)}, bf16[256,1408]{1,0:T(8,128)(2,1)S(1)}, u32[]{:S(2)}, u32[]{:S(2)}) %collective-permute-start.49) | collective-permute-done | bytes 720928 | tf_op jit(solution)/shard_map/ppermute | solution.py:45
  392.5 8.6 %collective-permute-done.45 = bf16[256,1408]{1,0:T(8,128)(2,1)S(1)} collective-permute-done((bf16[256,1408]{1,0:T(8,128)(2,1)S(1)}, bf16[256,1408]{1,0:T(8,128)(2,1)S(1)}, u32[]{:S(2)}, u32[]{:S(2)}) %collective-permute-start.45) | collective-permute-done | bytes 720928 | tf_op jit(solution)/shard_map/ppermute | solution.py:45
  417.0 17.5 %attn_bwd.1 = (bf16[512,512]{1,0:T(8,128)(2,1)}, bf16[512,512]{1,0:T(8,128)(2,1)}, bf16[512,512]{1,0:T(8,128)(2,1)}, bf16[512,512]{1,0:T(8,128)(2,1)}, bf16[512,...) custom-call(s32[20]{0:T(128)} %pad_add_fusion.1.refs_0_, ...), custom_call_target="tpu_custom_call" | custom-call | tf_op jit(solution)/shard_map/attn_bwd/pallas_call | solution.py:256
  436.2 8.6 %constant_dynamic-slice_fusion.4 = (bf16[512,4,1,256]{3,2,1,0:T(2,128)(2,1)}, bf16[512,4,1,256]{3,2,1,0:T(2,128)(2,1)}) fusion(bf16[512,4,2,256]{3,2,1,0:T(2,128)(2,1)} %reshape.260, s32[]{:T(128)S(6)} %select_n.249, s32[]{:T(128)S(6)} %select_n.248), kind=kLoop, calls=%fused_computation.189 | loop fusion | bytes 4194312 | tf_op jit(solution)/shard_map/jit(dynamic_index_in_dim)/dynamic_slice | solution.py:411
  485.1 7.1 %collective-permute-start.21 = (bf16[512,512]{1,0:T(8,128)(2,1)S(1)}, bf16[512,512]{1,0:T(8,128)(2,1)S(1)}, u32[]{:S(2)}, u32[]{:S(2)}) collective-permute-start(bf16[512,512]{1,0:T(8,128)(2,1)S(1)} %add_convert_fusion.4), channel_id=1, source_target_pairs={{0,8},{4,12},{8,16},{12,20},{16,24},{20,28},{24,0},{28,4},{1,9},{5... | collective-permute-start | bytes 1572872 | tf_op jit(solution)/shard_map/ppermute | solution.py:45
  501.9 15.6 %collective-permute-done.17 = bf16[512,512]{1,0:T(8,128)(2,1)S(1)} collective-permute-done((bf16[512,512]{1,0:T(8,128)(2,1)S(1)}, bf16[512,512]{1,0:T(8,128)(2,1)S(1)}, u32[]{:S(2)}, u32[]{:S(2)}) %collective-permute-start.17) | collective-permute-done | bytes 524320 | tf_op jit(solution)/shard_map/ppermute | solution.py:36
  518.5 6.4 %collective-permute-start.22 = (bf16[512,512]{1,0:T(8,128)(2,1)S(1)}, bf16[512,512]{1,0:T(8,128)(2,1)S(1)}, u32[]{:S(2)}, u32[]{:S(2)}) collective-permute-start(bf16[512,512]{1,0:T(8,128)(2,1)S(1)} %add_convert_fusion.3), channel_id=1, source_target_pairs={{0,8},{4,12},{8,16},{12,20},{16,24},{20,28},{24,0},{28,4},{1,9},{5... | collective-permute-start | bytes 1572872 | tf_op jit(solution)/shard_map/ppermute | solution.py:45
  553.4 11.5 %collective-permute-done.31 = bf16[512,512]{1,0:T(8,128)(2,1)S(1)} collective-permute-done((bf16[512,512]{1,0:T(8,128)(2,1)S(1)}, bf16[512,512]{1,0:T(8,128)(2,1)S(1)}, u32[]{:S(2)}, u32[]{:S(2)}) %collective-permute-start.31) | collective-permute-done | bytes 524320 | tf_op jit(solution)/shard_map/ppermute | solution.py:36
  587.1 9.0 %collective-permute-done.34 = bf16[256,512]{1,0:T(8,128)(2,1)S(1)} collective-permute-done((bf16[256,512]{1,0:T(8,128)(2,1)S(1)}, bf16[256,512]{1,0:T(8,128)(2,1)S(1)}, u32[]{:S(2)}, u32[]{:S(2)}) %collective-permute-start.34) | collective-permute-done | bytes 262176 | tf_op jit(solution)/shard_map/ppermute | solution.py:45
  (357 shorter events, 294.8 us)
Async XLA Ops:
  118.7 111.9 %collective-permute-start.54 = (bf16[512,1024]{0,1:T(8,128)(2,1)}, bf16[512,1024]{0,1:T(8,128)(2,1)}, u32[]{:S(2)}, u32[]{:S(2)}) collective-permute-start(bf16[512,1024]{0,1:T(8,128)(2,1)} %bitcast.19), channel_id=1, source_target_pairs={{0,4},{4,0},{8,12},{12,8},{16,20},{20,16},{24,28},{28,24},{1,5},{5... | collective-permute-start | bytes 3145736 | tf_op jit(solution)/shard_map/ppermute | solution.py:36
  185.8 57.5 %collective-permute-start.53 = (bf16[512,1408]{1,0:T(8,128)(2,1)}, bf16[512,1408]{1,0:T(8,128)(2,1)}, u32[]{:S(2)}, u32[]{:S(2)}) collective-permute-start(bf16[512,1408]{1,0:T(8,128)(2,1)} %get-tuple-element.53), channel_id=1, source_target_pairs={{0,4},{4,0},{8,12},{12,8},{16,20},{20,16},{24,28},{28,24},{1,5},{5... | collective-permute-start | bytes 4325384 | tf_op jit(solution)/shard_map/ppermute | solution.py:36
  191.6 114.7 %collective-permute-start.47 = (bf16[512,1408]{1,0:T(8,128)(2,1)}, bf16[512,1408]{1,0:T(8,128)(2,1)}, u32[]{:S(2)}, u32[]{:S(2)}) collective-permute-start(bf16[512,1408]{1,0:T(8,128)(2,1)} %get-tuple-element.51), channel_id=1, source_target_pairs={{0,4},{4,0},{8,12},{12,8},{16,20},{20,16},{24,28},{28,24},{1,5},{5... | collective-permute-start | bytes 4325384 | tf_op jit(solution)/shard_map/ppermute | solution.py:36
  197.8 34.3 %collective-permute-start.13 = (bf16[256,2048]{1,0:T(8,128)(2,1)}, bf16[256,2048]{1,0:T(8,128)(2,1)}, u32[]{:S(2)}, u32[]{:S(2)}) collective-permute-start(bf16[256,2048]{1,0:T(8,128)(2,1)} %fusion.4), channel_id=1, source_target_pairs={{0,1},{1,0},{2,3},{3,2},{4,5},{5,4},{6,7},{7,6},{8,9},{9,8},{10,11... | collective-permute-start | bytes 3145736 | tf_op jit(solution)/shard_map/ppermute | solution.py:32
  230.6 78.6 %collective-permute-start.43 = (bf16[512,1408]{1,0:T(8,128)(2,1)}, bf16[512,1408]{1,0:T(8,128)(2,1)S(1)}, u32[]{:S(2)}, u32[]{:S(2)}) collective-permute-start(bf16[512,1408]{1,0:T(8,128)(2,1)} %copy-done.47), channel_id=1, source_target_pairs={{0,4},{4,0},{8,12},{12,8},{16,20},{20,16},{24,28},{28,24},{1,5},{5... | collective-permute-start | bytes 4325384 | tf_op jit(solution)/shard_map/ppermute | solution.py:36
  232.2 72.6 %collective-permute-start.42 = (bf16[512,1024]{0,1:T(8,128)(2,1)}, bf16[512,1024]{0,1:T(8,128)(2,1)S(1)}, u32[]{:S(2)}, u32[]{:S(2)}) collective-permute-start(bf16[512,1024]{0,1:T(8,128)(2,1)} %bitcast.92), channel_id=1, source_target_pairs={{0,4},{4,0},{8,12},{12,8},{16,20},{20,16},{24,28},{28,24},{1,5},{5... | collective-permute-start | bytes 3145736 | tf_op jit(solution)/shard_map/ppermute | solution.py:36
  238.4 75.6 %collective-permute-start.14 = (bf16[256,2048]{1,0:T(8,128)(2,1)S(1)}, bf16[256,2048]{1,0:T(8,128)(2,1)S(1)}, u32[]{:S(2)}, u32[]{:S(2)}) collective-permute-start(bf16[256,2048]{1,0:T(8,128)(2,1)S(1)} %add_convert_fusion), channel_id=1, source_target_pairs={{0,2},{1,3},{2,0},{3,1},{4,6},{5,7},{6,4},{7,5},{8,10},{9,11},{10,... | collective-permute-start | bytes 3145736 | tf_op jit(solution)/shard_map/ppermute | solution.py:32
  243.3 231.9 %collective-permute-start.26 = (bf16[512,1024]{0,1:T(8,128)(2,1)}, bf16[512,1024]{0,1:T(8,128)(2,1)}, u32[]{:S(2)}, u32[]{:S(2)}) collective-permute-start(bf16[512,1024]{0,1:T(8,128)(2,1)} %bitcast.7), channel_id=1, source_target_pairs={{0,4},{4,0},{8,12},{12,8},{16,20},{20,16},{24,28},{28,24},{1,5},{5... | collective-permute-start | bytes 3145736 | tf_op jit(solution)/shard_map/ppermute | solution.py:36
  304.8 54.2 %collective-permute-start.11 = (bf16[256,2048]{1,0:T(8,128)(2,1)S(1)}, bf16[256,2048]{1,0:T(8,128)(2,1)S(1)}, u32[]{:S(2)}, u32[]{:S(2)}) collective-permute-start(bf16[256,2048]{1,0:T(8,128)(2,1)S(1)} %add_convert_fusion.2), channel_id=1, source_target_pairs={{0,2},{1,3},{2,0},{3,1},{4,6},{5,7},{6,4},{7,5},{8,10},{9,11},{10,... | collective-permute-start | bytes 3145736 | tf_op jit(solution)/shard_map/ppermute | solution.py:32
  309.2 33.3 %collective-permute-start.48 = (bf16[256,1408]{1,0:T(8,128)(2,1)S(1)}, bf16[256,1408]{1,0:T(8,128)(2,1)S(1)}, u32[]{:S(2)}, u32[]{:S(2)}) collective-permute-start(bf16[256,1408]{1,0:T(8,128)(2,1)S(1)} %convolution_convert_fusion.2), channel_id=1, source_target_pairs={{0,8},{4,12},{8,16},{12,20},{16,24},{20,28},{24,0},{28,4},{1,9},{5... | collective-permute-start | bytes 2162696 | tf_op jit(solution)/shard_map/ppermute | solution.py:45
  314.0 44.0 %collective-permute-start.44 = (bf16[256,1408]{1,0:T(8,128)(2,1)S(1)}, bf16[256,1408]{1,0:T(8,128)(2,1)S(1)}, u32[]{:S(2)}, u32[]{:S(2)}) collective-permute-start(bf16[256,1408]{1,0:T(8,128)(2,1)S(1)} %convolution_convert_fusion.3), channel_id=1, source_target_pairs={{0,8},{4,12},{8,16},{12,20},{16,24},{20,28},{24,0},{28,4},{1,9},{5... | collective-permute-start | bytes 2162696 | tf_op jit(solution)/shard_map/ppermute | solution.py:45
  329.9 73.1 %collective-permute-start.56 = (bf16[1408,256]{1,0:T(8,128)(2,1)S(1)}, bf16[1408,256]{1,0:T(8,128)(2,1)S(1)}, u32[]{:S(2)}, u32[]{:S(2)}) collective-permute-start(bf16[1408,256]{1,0:T(8,128)(2,1)S(1)} %fusion.12), channel_id=1, source_target_pairs={{0,8},{4,12},{8,16},{12,20},{16,24},{20,28},{24,0},{28,4},{1,9},{5... | collective-permute-start | bytes 2162696 | tf_op jit(solution)/shard_map/ppermute | solution.py:45
  345.3 43.5 %collective-permute-start.49 = (bf16[256,1408]{1,0:T(8,128)(2,1)S(1)}, bf16[256,1408]{1,0:T(8,128)(2,1)S(1)}, u32[]{:S(2)}, u32[]{:S(2)}) collective-permute-start(bf16[256,1408]{1,0:T(8,128)(2,1)S(1)} %fusion.10), channel_id=1, source_target_pairs={{0,8},{4,12},{8,16},{12,20},{16,24},{20,28},{24,0},{28,4},{1,9},{5... | collective-permute-start | bytes 2162696 | tf_op jit(solution)/shard_map/ppermute | solution.py:45
  358.9 42.1 %collective-permute-start.45 = (bf16[256,1408]{1,0:T(8,128)(2,1)S(1)}, bf16[256,1408]{1,0:T(8,128)(2,1)S(1)}, u32[]{:S(2)}, u32[]{:S(2)}) collective-permute-start(bf16[256,1408]{1,0:T(8,128)(2,1)S(1)} %fusion.8), channel_id=1, source_target_pairs={{0,8},{4,12},{8,16},{12,20},{16,24},{20,28},{24,0},{28,4},{1,9},{5... | collective-permute-start | bytes 2162696 | tf_op jit(solution)/shard_map/ppermute | solution.py:45
  361.9 47.0 %collective-permute-start.15 = (bf16[256,2048]{1,0:T(8,128)(2,1)S(1)}, bf16[256,2048]{1,0:T(8,128)(2,1)S(1)}, u32[]{:S(2)}, u32[]{:S(2)}) collective-permute-start(bf16[256,2048]{1,0:T(8,128)(2,1)S(1)} %get-tuple-element.45), channel_id=1, source_target_pairs={{0,1},{1,0},{2,3},{3,2},{4,5},{5,4},{6,7},{7,6},{8,9},{9,8},{10,11... | collective-permute-start | bytes 3145736 | tf_op jit(solution)/shard_map/ppermute | solution.py:32
  388.9 95.3 %collective-permute-start.12 = (bf16[256,2048]{1,0:T(8,128)(2,1)}, bf16[256,2048]{1,0:T(8,128)(2,1)}, u32[]{:S(2)}, u32[]{:S(2)}) collective-permute-start(bf16[256,2048]{1,0:T(8,128)(2,1)} %get-tuple-element.54), channel_id=1, source_target_pairs={{0,1},{1,0},{2,3},{3,2},{4,5},{5,4},{6,7},{7,6},{8,9},{9,8},{10,11... | collective-permute-start | bytes 3145736 | tf_op jit(solution)/shard_map/ppermute | solution.py:32
  401.1 56.4 %collective-permute-start.50 = (bf16[256,1408]{1,0:T(8,128)(2,1)}, bf16[256,1408]{1,0:T(8,128)(2,1)}, u32[]{:S(2)}, u32[]{:S(2)}) collective-permute-start(bf16[256,1408]{1,0:T(8,128)(2,1)} %fusion.9), channel_id=1, source_target_pairs={{0,8},{4,12},{8,16},{12,20},{16,24},{20,28},{24,0},{28,4},{1,9},{5... | collective-permute-start | bytes 2162696 | tf_op jit(solution)/shard_map/ppermute | solution.py:45
  403.0 62.5 %collective-permute-start.46 = (bf16[256,1408]{1,0:T(8,128)(2,1)}, bf16[256,1408]{1,0:T(8,128)(2,1)}, u32[]{:S(2)}, u32[]{:S(2)}) collective-permute-start(bf16[256,1408]{1,0:T(8,128)(2,1)} %fusion.7), channel_id=1, source_target_pairs={{0,8},{4,12},{8,16},{12,20},{16,24},{20,28},{24,0},{28,4},{1,9},{5... | collective-permute-start | bytes 2162696 | tf_op jit(solution)/shard_map/ppermute | solution.py:45
  472.6 45.8 %collective-permute-start.57 = (bf16[1408,256]{1,0:T(8,128)(2,1)S(1)}, bf16[1408,256]{1,0:T(8,128)(2,1)S(1)}, u32[]{:S(2)}, u32[]{:S(2)}) collective-permute-start(bf16[1408,256]{1,0:T(8,128)(2,1)S(1)} %copy-done.54), channel_id=1, source_target_pairs={{0,8},{4,12},{8,16},{12,20},{16,24},{20,28},{24,0},{28,4},{1,9},{5... | collective-permute-start | bytes 2162696 | tf_op jit(solution)/shard_map/ppermute | solution.py:45
  475.3 53.4 %collective-permute-start.38 = (bf16[512,1024]{0,1:T(8,128)(2,1)S(1)}, bf16[512,1024]{0,1:T(8,128)(2,1)S(1)}, u32[]{:S(2)}, u32[]{:S(2)}) collective-permute-start(bf16[512,1024]{0,1:T(8,128)(2,1)S(1)} %bitcast.91), channel_id=1, source_target_pairs={{0,4},{4,0},{8,12},{12,8},{16,20},{20,16},{24,28},{28,24},{1,5},{5... | collective-permute-start | bytes 3145736 | tf_op jit(solution)/shard_map/ppermute | solution.py:36
  483.9 33.7 %collective-permute-start.17 = (bf16[512,512]{1,0:T(8,128)(2,1)S(1)}, bf16[512,512]{1,0:T(8,128)(2,1)S(1)}, u32[]{:S(2)}, u32[]{:S(2)}) collective-permute-start(bf16[512,512]{1,0:T(8,128)(2,1)S(1)} %copy-done.56), channel_id=1, source_target_pairs={{0,4},{4,0},{8,12},{12,8},{16,20},{20,16},{24,28},{28,24},{1,5},{5... | collective-permute-start | bytes 1572872 | tf_op jit(solution)/shard_map/ppermute | solution.py:36
  485.1 33.1 %collective-permute-start.21 = (bf16[512,512]{1,0:T(8,128)(2,1)S(1)}, bf16[512,512]{1,0:T(8,128)(2,1)S(1)}, u32[]{:S(2)}, u32[]{:S(2)}) collective-permute-start(bf16[512,512]{1,0:T(8,128)(2,1)S(1)} %add_convert_fusion.4), channel_id=1, source_target_pairs={{0,8},{4,12},{8,16},{12,20},{16,24},{20,28},{24,0},{28,4},{1,9},{5... | collective-permute-start | bytes 1572872 | tf_op jit(solution)/shard_map/ppermute | solution.py:45
  532.2 44.6 %collective-permute-start.30 = (bf16[256,512]{1,0:T(8,128)(2,1)}, bf16[256,512]{1,0:T(8,128)(2,1)}, u32[]{:S(2)}, u32[]{:S(2)}) collective-permute-start(bf16[256,512]{1,0:T(8,128)(2,1)} %fusion.24), channel_id=1, source_target_pairs={{0,8},{4,12},{8,16},{12,20},{16,24},{20,28},{24,0},{28,4},{1,9},{5... | collective-permute-start | bytes 786440 | tf_op jit(solution)/shard_map/ppermute | solution.py:45
  551.1 35.3 %collective-permute-start.40 = (bf16[512,256]{1,0:T(8,128)(2,1)S(1)}, bf16[512,256]{1,0:T(8,128)(2,1)S(1)}, u32[]{:S(2)}, u32[]{:S(2)}) collective-permute-start(bf16[512,256]{1,0:T(8,128)(2,1)S(1)} %fusion.29), channel_id=1, source_target_pairs={{0,8},{4,12},{8,16},{12,20},{16,24},{20,28},{24,0},{28,4},{1,9},{5... | collective-permute-start | bytes 786440 | tf_op jit(solution)/shard_map/ppermute | solution.py:45
  (101 other events, 1515.5 us)

commit v2 on v1

--- a/solution.py
+++ b/solution.py
@@ -18,6 +18,7 @@
 F32 = jnp.float32
 NT = (((1,), (1,)), ((), ()))
 TN = (((0,), (0,)), ((), ()))
+NN = (((1,), (0,)), ((), ()))
 VM = pl.BlockSpec(memory_space=pltpu.VMEM)
 SM = pl.BlockSpec(memory_space=pltpu.SMEM)
 ANY = pl.BlockSpec(memory_space=pl.ANY)
@@ -88,6 +89,7 @@
                 pl.BlockSpec((half, 2 * wk.shape[1]), lambda i, c: (i, 0)),
             ],
         ),
+        cost_estimate=pl.CostEstimate(flops=int(2.9e9), bytes_accessed=0, transcendentals=0),
         name="norm_kv",
     )(core, tokens, gain, wk, wv, cosine, sine)
 
@@ -113,9 +115,7 @@
             pl.BlockSpec((half, HD), lambda i: (i, 0)),
         ],
         out_specs=pl.BlockSpec((half, w.shape[1]), lambda i: (i, 0)),
-        cost_estimate=pl.CostEstimate(
-            flops=2 * rows * width * w.shape[1], bytes_accessed=6 << 20, transcendentals=0
-        ),
+        cost_estimate=pl.CostEstimate(flops=int(2.9e9), bytes_accessed=0, transcendentals=0),
         name="query_proj",
     )(x, w, cosine, sine)
 
@@ -195,6 +195,7 @@
             pltpu.VMEM((HD, rows), F32),
             pltpu.SemaphoreType.DMA((len(slots),)),
         ],
+        cost_estimate=pl.CostEstimate(flops=int(5.2e9), bytes_accessed=0, transcendentals=0),
         name="attn_fwd",
     )(meta, q, pos, low, *slots)
 
@@ -265,15 +266,340 @@
             pltpu.VMEM((rows, HD), F32),
             pltpu.SemaphoreType.DMA((count,)),
         ],
+        cost_estimate=pl.CostEstimate(flops=int(7.2e9), bytes_accessed=0, transcendentals=0),
         name="attn_bwd",
     )(meta, q, pos, low, lse, mixed, dmix, cosine, sine, *slots)
     return outs[0], outs[1:]
+
+
+def cost(micros):
+    return pl.CostEstimate(flops=int(micros * 0.575e9), bytes_accessed=0, transcendentals=0)
+
+
+def split_rows(total, own_ref, other_ref):
+    half = own_ref.shape[0]
+    own_ref[...] = total[:half].astype(BF)
+    other_ref[...] = total[half:].astype(BF)
+
+
+def project_kernel(spec, *refs):
+    total = None
+    for a, b, offset, dims in spec:
+        left = refs[a][...] if dims is not None else None
+        if dims == "nt":
+            right, form = refs[b][:, offset : offset + left.shape[1]], NT
+        else:
+            right, form = refs[b][offset : offset + left.shape[1], :], NN
+        term = dot(left, right, form)
+        total = term if total is None else total + term
+    split_rows(total, refs[-2], refs[-1])
+
+
+def project(pairs, dims, tile, micros):
+    operands, specs, plan, weights = [], [], [], []
+    for a, b, offset in pairs:
+        operands.append(a)
+        specs.append(pl.BlockSpec(a.shape, lambda i: (0, 0)))
+        spot = next((at for at, seen in weights if seen is b), None)
+        left = len(operands) - 1
+        if spot is None:
+            spot = len(operands)
+            operands.append(b)
+            weights.append((spot, b))
+            if dims == "nt":
+                specs.append(pl.BlockSpec((tile, b.shape[1]), lambda i: (i, 0)))
+            else:
+                specs.append(pl.BlockSpec((b.shape[0], tile), lambda i: (0, i)))
+        plan.append((left, spot, offset, dims))
+    rows = pairs[0][0].shape[0]
+    width = pairs[0][1].shape[0 if dims == "nt" else 1]
+    return pl.pallas_call(
+        functools.partial(project_kernel, plan),
+        out_shape=[jax.ShapeDtypeStruct((rows // 2, width), BF)] * 2,
+        grid=(width // tile,),
+        in_specs=specs,
+        out_specs=[pl.BlockSpec((rows // 2, tile), lambda i: (0, i))] * 2,
+        cost_estimate=cost(micros),
+        name="project",
+    )(*operands)
+
+
+def back_dense_kernel(first_ref, second_ref, wg_ref, wu_ref, own_ref, other_ref):
+    total = None
+    offset = 0
+    for ref in (first_ref, second_ref):
+        count = ref.shape[2]
+        for k, w_ref in enumerate((wg_ref, wu_ref)):
+            term = dot(ref[k], w_ref[:, offset : offset + count], NT)
+            total = term if total is None else total + term
+        offset += count
+    split_rows(total, own_ref, other_ref)
+
+
+def back_dense(first, second, w_gate, w_up, tile):
+    width, hidden = w_gate.shape
+    rows = first.shape[1]
+    whole = lambda v: pl.BlockSpec(v.shape, lambda i: (0, 0, 0))
+    weight = pl.BlockSpec((tile, hidden), lambda i: (i, 0))
+    return pl.pallas_call(
+        back_dense_kernel,
+        out_shape=[jax.ShapeDtypeStruct((rows // 2, width), BF)] * 2,
+        grid=(width // tile,),
+        in_specs=[whole(first), whole(second), weight, weight],
+        out_specs=[pl.BlockSpec((rows // 2, tile), lambda i: (0, i))] * 2,
+        cost_estimate=cost(11),
+        name="back_dense",
+    )(first, second, w_gate, w_up)
+
+
+def gated_kernel(own_ref, other_ref, wg_ref, wu_ref, di_ref, inner_ref, dgu_ref, all_ref):
+    @pl.when(pl.program_id(0) == 0)
+    def _():
+        half = own_ref.shape[0]
+        all_ref[:half, :] = own_ref[...]
+        all_ref[half:, :] = other_ref[...]
+
+    gate = dot(all_ref[...], wg_ref[...])
+    up = dot(all_ref[...], wu_ref[...])
+    sigma = 1.0 / (1.0 + jnp.exp(-gate))
+    silu = gate * sigma
+    d_inner = di_ref[...]
+    inner_ref[...] = (silu * up).astype(BF)
+    dgu_ref[0] = (d_inner * up * sigma * (1.0 + gate * (1.0 - sigma))).astype(BF)
+    dgu_ref[1] = (d_inner * silu).astype(BF)
+
+
+def gated(own, other, wg, wu, d_inner, first, columns, tile):
+    half, width = own.shape
+    weight = pl.BlockSpec((width, tile), lambda i: (0, first // tile + i))
+    whole = pl.BlockSpec((half, width), lambda i: (0, 0))
+    return pl.pallas_call(
+        gated_kernel,
+        out_shape=[
+            jax.ShapeDtypeStruct((2 * half, columns), BF),
+            jax.ShapeDtypeStruct((2, 2 * half, columns), BF),
+        ],
+        grid=(pl.cdiv(columns, tile),),
+        in_specs=[
+            whole,
+            whole,
+            weight,
+            weight,
+            pl.BlockSpec((2 * half, tile), lambda i: (0, first // tile + i)),
+        ],
+        out_specs=[
+            pl.BlockSpec((2 * half, tile), lambda i: (0, i)),
+            pl.BlockSpec((2, 2 * half, tile), lambda i: (0, 0, i)),
+        ],
+        scratch_shapes=[pltpu.VMEM((2 * half, width), BF)],
+        cost_estimate=cost(7.5),
+        name="gated",
+    )(own, other, wg, wu, d_inner)
+
+
+def mixed_grad_kernel(own_ref, other_ref, w_ref, out_ref):
+    both = jnp.concatenate([own_ref[...], other_ref[...]], axis=0)
+    out_ref[...] = dot(both, w_ref[...], NT).astype(BF)
+
+
+def mixed_grad(own, other, w):
+    return pl.pallas_call(
+        mixed_grad_kernel,
+        out_shape=jax.ShapeDtypeStruct((2 * own.shape[0], w.shape[0]), BF),
+        in_specs=[VM] * 3,
+        out_specs=VM,
+        cost_estimate=cost(4),
+        name="mixed_grad",
+    )(own, other, w)
+
+
+def d_inner_kernel(x_ref, w_ref, out_ref):
+    out_ref[...] = dot(x_ref[...], w_ref[...], NT)
+
+
+def inner_grad(x, w, tile):
+    rows, width = x.shape
+    hidden = w.shape[0]
+    return pl.pallas_call(
+        d_inner_kernel,
+        out_shape=jax.ShapeDtypeStruct((rows, hidden), F32),
+        grid=(pl.cdiv(hidden, tile),),
+        in_specs=[
+            pl.BlockSpec((rows, width), lambda i: (0, 0)),
+            pl.BlockSpec((tile, width), lambda i: (i, 0)),
+        ],
+        out_specs=pl.BlockSpec((rows, tile), lambda i: (0, i)),
+        cost_estimate=cost(8),
+        name="inner_grad",
+    )(x, w)
+
+
+def pack_kernel(count, plan, strip, tbl, *refs):
+    ins, outs = refs[:count], refs[count:]
+    for out_ref, pieces in zip(outs, plan):
+        column = 0
+        for at, rows, row in pieces:
+            for k in range(tbl.shape[1]):
+                first = pl.multiple_of(tbl[row, k] * strip, 128)
+                out_ref[:, column : column + strip] = ins[at][rows, pl.ds(first, strip)]
+                column += strip
+
+
+def pack(values, plan, tbl, strip):
+    turns = tbl.shape[1]
+    if strip % 128:
+        cut = lambda v, rows, at: lax.dynamic_slice_in_dim(v[rows], at * strip, strip, axis=1)
+        return [
+            jnp.concatenate(
+                [cut(values[at], rows, tbl[row, k]) for at, rows, row in pieces for k in range(turns)],
+                axis=1,
+            )
+            for pieces in plan
+        ]
+    return pl.pallas_call(
+        functools.partial(pack_kernel, len(values), plan, strip),
+        out_shape=[
+            jax.ShapeDtypeStruct(
+                (p[0][1].stop - p[0][1].start, len(p) * turns * strip), values[0].dtype
+            )
+            for p in plan
+        ],
+        in_specs=[SM] + [VM] * len(values),
+        out_specs=[VM] * len(plan),
+        cost_estimate=cost(1.5),
+        name="pack",
+    )(tbl, *values)
+
+
+def strip_rows_kernel(halves, near, rights, nears, tbl, *refs):
+    left = refs[:halves]
+    left_near = refs[halves : halves + near]
+    right = refs[halves + near : halves + near + rights]
+    right_near = refs[halves + near + rights : halves + near + rights + nears]
+    outs = refs[halves + near + rights + nears :]
+    step = pl.program_id(0)
+    join = lambda group: (
+        group[0][...] if len(group) == 1 else jnp.concatenate([r[...] for r in group], axis=0)
+    )
+    mine, theirs = join(left), join(left_near)
+    pieces = []
+    for r, n in zip(right, right_near):
+        planes = range(r.shape[0]) if len(r.shape) == 3 else [None]
+        for k in planes:
+            a = r[...] if k is None else r[k]
+            b = n[...] if k is None else n[k]
+            pieces.append((dot(mine, a, TN) + dot(theirs, b, TN)).astype(BF))
+    for k, out in enumerate(outs):
+
+        @pl.when(step == k)
+        def _():
+            column = 0
+            for piece in pieces:
+                out[:, column : column + piece.shape[1]] = piece
+                column += piece.shape[1]
+
+
+def strip_rows_grad(left, left_near, right, right_near, tbl, strip, micros):
+    turns = tbl.shape[1]
+    columns = sum(r.shape[-1] * (r.shape[0] if r.ndim == 3 else 1) for r in right)
+    if strip % 128:
+        near = jnp.concatenate(left_near, axis=0)
+        mine = jnp.concatenate(left, axis=0)
+        flat = lambda r: [r] if r.ndim == 2 else [r[k] for k in range(r.shape[0])]
+        outs = []
+        for k in range(turns):
+            a = lax.dynamic_slice_in_dim(mine, tbl[0, k] * strip, strip, axis=1)
+            b = near[:, k * strip : (k + 1) * strip]
+            outs.append(
+                jnp.concatenate(
+                    [
+                        dot(a, x, TN) + dot(b, y, TN)
+                        for r, n in zip(right, right_near)
+                        for x, y in zip(flat(r), flat(n))
+                    ],
+                    axis=1,
+                ).astype(BF)
+            )
+        return outs
+    whole = lambda v: pl.BlockSpec(v.shape, lambda i, t: (0,) * v.ndim)
+    return pl.pallas_call(
+        functools.partial(
+            strip_rows_kernel, len(left), len(left_near), len(right), len(right_near)
+        ),
+        out_shape=[jax.ShapeDtypeStruct((strip, columns), BF)] * turns,
+        grid_spec=pltpu.PrefetchScalarGridSpec(
+            num_scalar_prefetch=1,
+            grid=(turns,),
+            in_specs=[pl.BlockSpec((v.shape[0], strip), lambda i, t: (0, t[0, i])) for v in left]
+            + [pl.BlockSpec((v.shape[0], strip), lambda i, t: (0, i)) for v in left_near]
+            + [whole(v) for v in [*right, *right_near]],
+            out_specs=[pl.BlockSpec((strip, columns), lambda i, t: (0, 0))] * turns,
+        ),
+        cost_estimate=cost(micros),
+        name="strip_rows",
+    )(tbl, *left, *left_near, *right, *right_near)
+
+
+def strip_columns_kernel(halves, near, strip, *refs):
+    left_ref, left_near_ref = refs[:2]
+    right = refs[2 : 2 + halves]
+    right_near = refs[2 + halves : 2 + halves + near]
+    outs = refs[2 + halves + near :]
+    total = None
+    for ref, group in ((left_ref, right), (left_near_ref, right_near)):
+        row = 0
+        for r in group:
+            term = dot(ref[row : row + r.shape[0], :], r[...], TN)
+            total = term if total is None else total + term
+            row += r.shape[0]
+    for k, out in enumerate(outs):
+        out[...] = total[:, k * strip : (k + 1) * strip].astype(BF)
+
+
+def strip_columns_grad(left, left_near, right, right_near, turns, strip, tile, micros):
+    rows, count = left.shape
+    whole = lambda v: pl.BlockSpec(v.shape, lambda i: (0, 0))
+    return pl.pallas_call(
+        functools.partial(strip_columns_kernel, len(right), len(right_near), strip),
+        out_shape=[jax.ShapeDtypeStruct((count, strip), BF)] * turns,
+        grid=(pl.cdiv(count, tile),),
+        in_specs=[pl.BlockSpec((rows, tile), lambda i: (0, i))] * 2
+        + [whole(v) for v in [*right, *right_near]],
+        out_specs=[pl.BlockSpec((tile, strip), lambda i: (i, 0))] * turns,
+        cost_estimate=cost(micros),
+        name="strip_columns",
+    )(left, left_near, *right, *right_near)
+
+
+def close_kv_kernel(a_ref, b_ref, c_ref, cos_ref, sin_ref, dk_ref, dv_ref):
+    total = a_ref[...].astype(F32) + b_ref[...].astype(F32) + c_ref[...].astype(F32)
+    width = dk_ref.shape[1]
+    for h in range(width // HD):
+        cols = slice(h * HD, (h + 1) * HD)
+        dk_ref[:, cols] = rope(total[:, cols], cos_ref[...], -sin_ref[...]).astype(BF)
+    dv_ref[...] = total[:, width:].astype(BF)
+
+
+def close_kv(a, b, c, cosine, sine):
+    rows, width = a.shape
+    return pl.pallas_call(
+        close_kv_kernel,
+        out_shape=[jax.ShapeDtypeStruct((rows, width // 2), BF)] * 2,
+        in_specs=[VM] * 5,
+        out_specs=[VM] * 2,
+        cost_estimate=cost(1.5),
+        name="close_kv",
+    )(a, b, c, cosine, sine)
 
 
 def norm_backward(source, scale_rows, gain, upstream):
     weighted = upstream * gain
     average = jnp.mean(weighted * source, axis=1, keepdims=True)
     return scale_rows * weighted - source * scale_rows**3 * average
+
+
+def after(value, *done):
+    return lax.optimization_barrier((value, *done))[0]
 
 
 def shards(
@@ -300,7 +626,7 @@
     wide_index = lax.axis_index("wide")
     member = wide_index % group
     seq_index = wide_index // group
-    side = wide_index % 2
+    side = (wide_index % 2).astype(jnp.int32)
     core = lax.axis_index("narrow") % 2
     strip = width // wide
     turns = wide // 2
@@ -347,153 +673,227 @@
     pos_row = pos[None, :]
     low_row = low[None, :]
 
+    turn_row = (wide_index // 2 - 1 - jnp.arange(turns, dtype=jnp.int32)) % turns
+    tbl = jnp.stack([2 * turn_row + side, 2 * turn_row + 1 - side]).astype(jnp.int32)
     core_arr = core.astype(jnp.int32)[None]
     normed_one, both = norm_kv(core_arr, tokens, gain_attn[None, :], w_key, w_value, cosine, sine)
-    near = [both]
-    far = [wide_swap(both)]
-    for step in range(1, ring):
-        near.append(wide_ring(near[-1], group))
-        far.append(wide_swap(near[-1]))
+    near, far = [both], []
+    low_rows, all_rows = slice(0, half), slice(0, rows)
+
+    def together(*values):
+        return list(lax.optimization_barrier(values))
+
+    query = d_dense = d_inner = input_near = d_dense_strips = None
+    for step in range(ring):
+        held = near[step]
+        group_out = [wide_swap(held)]
+        if step + 1 < ring:
+            group_out.append(wide_ring(held, group))
+        if step == 0:
+            query = query_proj(normed_one, w_query, cosine, sine)
+            keep_rel = jnp.concatenate([own_half(keep_mask), other_half(keep_mask)])[:, None]
+            cot_rel = jnp.concatenate([own_half(cotangent), other_half(cotangent)])
+            d_dense = jnp.where(keep_rel > 0, cot_rel, jnp.zeros_like(cot_rel))
+            group_out += [query, d_dense]
+        if step == 1:
+            d_inner = inner_grad(d_dense, w_down, 256)
+            group_out += [d_inner]
+        if step == 2:
+            input_near, d_dense_strips = pack(
+                [normed_one, d_dense],
+                [[(0, low_rows, 1), (1, low_rows, 1)], [(1, all_rows, 0)]],
+                tbl,
+                strip,
+            )
+            group_out += [input_near, d_dense_strips]
+        group_out = together(*group_out)
+        far.append(group_out[0])
+        if step + 1 < ring:
+            near.append(group_out[1])
+        if step == 0:
+            query, d_dense = group_out[-2:]
+        if step == 1:
+            d_inner = group_out[-1]
+        if step == 2:
+            input_near, d_dense_strips = group_out[-2:]
     slots = near + far
-    query = query_proj(normed_one, w_query, cosine, sine)
     mixed, lse = attn_fwd(meta, query, pos_row, low_row, slots)
 
-    def reduce_narrow(other_part, own_part):
+    def reduce_narrow(halves, hold=()):
+        own_part, other_part = halves
         got = narrow_swap(other_part, 1)
-        held = (own_part + got.astype(F32)).astype(BF)
-        return held.astype(F32) + narrow_swap(held, 2).astype(F32)
-
-    def cut(value):
-        return value[:half], value[half:]
-
-    mixed_own, mixed_other = cut(mixed)
-    attn_out = reduce_narrow(dot(mixed_other, w_out).astype(BF), dot(mixed_own, w_out))
+        held = (own_part.astype(F32) + got.astype(F32)).astype(BF)
+        return held, narrow_swap(held, 2)
+
+    def total_of(held, got):
+        return held.astype(F32) + got.astype(F32)
+
+    input_near = wide_swap(after(input_near, far[-1], mixed))
+    held, got = reduce_narrow(project([(mixed, w_out, 0)], "nn", 1024, 4))
+    got, input_near = together(got, input_near)
+    input_near_other = narrow_swap(input_near, 1)
+    mixed_near = wide_swap(after(mixed, input_near))
     source = own_half(tokens).astype(F32)
     keep_own = own_half(keep_mask).astype(F32)[:, None]
-    hidden_one = source + keep_own * attn_out
+    hidden_one = source + keep_own * total_of(held, got)
     gain_two = gain_dense.astype(F32)
     scale_two = lax.rsqrt(jnp.mean(hidden_one * hidden_one, axis=1, keepdims=True) + EPSILON)
-    normed_two_own = (hidden_one * scale_two * gain_two).astype(BF)
-    normed_two = jnp.concatenate([normed_two_own, narrow_swap(normed_two_own, 1)], axis=0)
-
-    keep_rel = jnp.concatenate([own_half(keep_mask), other_half(keep_mask)])[:, None]
-    cot_rel = jnp.concatenate([own_half(cotangent), other_half(cotangent)])
-    d_dense = jnp.where(keep_rel > 0, cot_rel, jnp.zeros_like(cot_rel))
-    d_inner = dot(d_dense, w_down, NT)
-    gate = dot(normed_two, w_gate)
-    up = dot(normed_two, w_up)
-    sigma = jax.nn.sigmoid(gate)
-    silu = gate * sigma
-    inner = (silu * up).astype(BF)
-    d_gate = (d_inner * up * sigma * (1.0 + gate * (1.0 - sigma))).astype(BF)
-    d_up = (d_inner * silu).astype(BF)
-
-    dg_own, dg_other = cut(d_gate)
-    du_own, du_other = cut(d_up)
-
-    def back_dense(dg, du):
-        return dot(dg, w_gate, NT) + dot(du, w_up, NT)
-
-    d_normed_two = reduce_narrow(back_dense(dg_other, du_other).astype(BF), back_dense(dg_own, du_own))
-    inner_own, inner_other = cut(inner)
-    dense_out = reduce_narrow(dot(inner_other, w_down).astype(BF), dot(inner_own, w_down))
-    output_own = (hidden_one + keep_own * dense_out).astype(BF)
+    normed_two = (hidden_one * scale_two * gain_two).astype(BF)
+    normed_two_other = narrow_swap(normed_two, 1)
+    (normed_two_near,) = pack([normed_two], [[(0, low_rows, 1)]], tbl, strip)
+    normed_two_near = wide_swap(after(normed_two_near, mixed_near))
+    normed_two_near_other = narrow_swap(normed_two_near, 1)
+
+    hidden = w_gate.shape[1]
+    tile = 256
+    first_count = 3 * tile
+    inner_a, dgu_a = gated(
+        normed_two, normed_two_other, w_gate, w_up, d_inner, 0, first_count, tile
+    )
+    inner_a_near = wide_swap(after(inner_a, normed_two_near))
+    inner_b, dgu_b = gated(
+        after(normed_two, inner_a),
+        normed_two_other,
+        w_gate,
+        w_up,
+        d_inner,
+        first_count,
+        hidden - first_count,
+        tile,
+    )
+    back = back_dense(dgu_a, dgu_b, w_gate, w_up, 512)
+    held, got = reduce_narrow(back)
+
+    def ring_sum(parts, start=None):
+        carried = parts[0] if start is None else after(parts[0], start)
+        for k, part in enumerate(parts[1:]):
+            carried = wide_ring(carried, wide)
+            total = part.astype(F32) + carried.astype(F32)
+            carried = total.astype(BF)
+        return total
+
+    d_dense_near = [input_near[:, turns * strip :], input_near_other[:, turns * strip :]]
+    normed_one_near = [input_near[:, : turns * strip], input_near_other[:, : turns * strip]]
+    down_a = strip_columns_grad(
+        inner_a, inner_a_near, [d_dense_strips], d_dense_near, turns, strip, tile, 4
+    )
+    inner_b_near = wide_swap(after(inner_b, inner_a_near))
+    grad_down_a = ring_sum(down_a)
+    dgu_a_near = wide_swap(after(dgu_a, inner_b_near))
+    down_b = strip_columns_grad(
+        inner_b, inner_b_near, [d_dense_strips], d_dense_near, turns, strip, tile, 4
+    )
+    grad_down_b = ring_sum(down_b)
+
+    upstream = own_half(cotangent).astype(F32)
+    d_hidden = upstream + norm_backward(hidden_one, scale_two, gain_two, total_of(held, got))
+    d_attn = (keep_own * d_hidden).astype(BF)
+    d_attn_other = narrow_swap(d_attn, 1)
+
+    d_mixed = mixed_grad(d_attn, d_attn_other, w_out)
+    d_query, d_slots = attn_bwd(
+        meta, query, pos_row, low_row, lse, mixed, d_mixed, cosine, sine, slots
+    )
+    dense_parts = project([(inner_a, w_down, 0), (inner_b, w_down, first_count)], "nn", 512, 6)
+    held_out, got_out = reduce_narrow((dense_parts[0], after(dense_parts[1], d_mixed)))
+    output_own = (hidden_one + keep_own * total_of(held_out, got_out)).astype(BF)
     output = ordered(output_own, narrow_swap(output_own, 1))
 
-    upstream = own_half(cotangent).astype(F32)
-    d_hidden = upstream + norm_backward(hidden_one, scale_two, gain_two, d_normed_two)
-    d_attn_own = (keep_own * d_hidden).astype(BF)
-    d_attn = jnp.concatenate([d_attn_own, narrow_swap(d_attn_own, 1)], axis=0)
-
-    def strips(value):
-        cells = value.reshape(value.shape[0], turns, 2, strip)
-        mine = lax.dynamic_index_in_dim(cells, side, 2, keepdims=False)
-        theirs = lax.dynamic_index_in_dim(cells, 1 - side, 2, keepdims=False)
-        flat = (value.shape[0], turns * strip)
-        return jnp.concatenate([mine.reshape(flat), wide_swap(theirs.reshape(flat))], axis=0)
-
-    def paired(value):
-        return jnp.concatenate([value, wide_swap(value)], axis=0)
-
-    def ring_sum(part):
-        carried = None
-        for step in range(1, turns + 1):
-            piece = part((wide_index // 2 - step) % turns)
+    carried = theirs = None
+    for step in [*range(1, ring), 0]:
+        sent = d_slots[ring + step]
+        theirs = wide_swap(sent if theirs is None else after(sent, theirs))
+        if step:
+            piece = d_slots[step].astype(F32) + theirs.astype(F32)
             if carried is not None:
                 piece = piece + carried.astype(F32)
-            if step == turns:
-                return piece
-            carried = wide_ring(piece.astype(BF), wide)
-
-    def strip_of(value, turn):
-        return lax.dynamic_slice_in_dim(value, turn * strip, strip, axis=1)
-
-    d_dense_strips = strips(d_dense)
-    normed_two_strips = strips(normed_two)
-    normed_one_strips = strips(normed_one)
-    d_attn_strips = strips(d_attn)
-    inner_two = paired(inner)
-    d_gate_two = paired(d_gate)
-    d_up_two = paired(d_up)
-    grad_down = ring_sum(lambda t: dot(inner_two, strip_of(d_dense_strips, t), TN))
-    grad_gate = ring_sum(lambda t: dot(strip_of(normed_two_strips, t), d_gate_two, TN))
-    grad_up = ring_sum(lambda t: dot(strip_of(normed_two_strips, t), d_up_two, TN))
-
-    d_mixed = dot(d_attn, w_out, NT).astype(BF)
-    d_query, d_slots = attn_bwd(
-        meta, query, pos_row, low_row, lse, mixed, d_mixed, cosine, sine, slots
-    )
-    mixed_two = paired(mixed)
-    grad_out = ring_sum(lambda t: dot(mixed_two, strip_of(d_attn_strips, t), TN))
-
-    carried = None
-    for step in [*range(1, ring), 0]:
-        piece = d_slots[step].astype(F32) + wide_swap(d_slots[ring + step]).astype(F32)
-        if carried is not None:
-            piece = piece + carried.astype(F32)
-        if step:
             carried = wide_ring(piece.astype(BF), group)
+    d_key, d_value = close_kv(d_slots[0], theirs, carried, cosine, sine)
+
+    normed_two_sides = [normed_two_near, normed_two_near_other]
+    gate_up_a = strip_rows_grad(
+        [normed_two, normed_two_other], normed_two_sides, [dgu_a], [dgu_a_near], tbl, strip, 8
+    )
+    grad_gate_up_a = ring_sum(gate_up_a)
+    d_query_near = wide_swap(d_query)
+    dgu_b_near = wide_swap(after(dgu_b, dgu_a_near))
+    gate_up_b = strip_rows_grad(
+        [normed_two, normed_two_other], normed_two_sides, [dgu_b], [dgu_b_near], tbl, strip, 7
+    )
+    grad_gate_up_b = ring_sum(gate_up_b)
+    d_attn_near, d_attn_strips, d_attn_other_strips = pack(
+        [d_attn, d_attn_other],
+        [[(0, low_rows, 1)], [(0, low_rows, 0)], [(1, low_rows, 0)]],
+        tbl,
+        strip,
+    )
+    d_attn_near = wide_swap(after(d_attn_near, dgu_b_near))
+    d_attn_near_other = narrow_swap(d_attn_near, 1)
+    grad_out = ring_sum(
+        strip_columns_grad(
+            mixed,
+            mixed_near,
+            [d_attn_strips, d_attn_other_strips],
+            [d_attn_near, d_attn_near_other],
+            turns,
+            strip,
+            tile,
+            4,
+        )
+    )
+    grad_query = ring_sum(
+        strip_rows_grad([normed_one], normed_one_near, [d_query], [d_query_near], tbl, strip, 4)
+    )
+
     kv_width = w_key.shape[1]
-    d_keys = piece[:, :kv_width].reshape(rows, kv_width // HD, HD)
-    turned = jnp.concatenate([d_keys[..., HD // 2 :], d_keys[..., : HD // 2]], axis=-1)
-    d_keys = d_keys * cosine[:, None, :] - turned * sine[:, None, :]
-    d_kv = jnp.concatenate([d_keys.reshape(rows, kv_width), piece[:, kv_width:]], axis=1).astype(BF)
-    d_key, d_value = d_kv[:, :kv_width], d_kv[:, kv_width:]
-
-    def back_attn(part):
-        return (
-            dot(part(d_query), w_query, NT)
-            + dot(part(d_key), w_key, NT)
-            + dot(part(d_value), w_value, NT)
-        )
-
-    d_normed_one = reduce_narrow(
-        back_attn(lambda v: v[half:]).astype(BF), back_attn(lambda v: v[:half])
+    held, got = reduce_narrow(
+        project([(d_query, w_query, 0), (d_key, w_key, 0), (d_value, w_value, 0)], "nt", 512, 6)
     )
     gain_one = gain_attn.astype(F32)
     scale_one = lax.rsqrt(jnp.mean(source * source, axis=1, keepdims=True) + EPSILON)
+    d_normed_one = total_of(held, got)
     grad_own = (d_hidden + norm_backward(source, scale_one, gain_one, d_normed_one)).astype(BF)
     grad_tokens = ordered(grad_own, narrow_swap(grad_own, 1))
 
-    d_query_two = paired(d_query)
-    d_kv_two = paired(d_kv)
-    grad_query = ring_sum(lambda t: dot(strip_of(normed_one_strips, t), d_query_two, TN))
-    grad_kv = ring_sum(lambda t: dot(strip_of(normed_one_strips, t), d_kv_two, TN))
+    d_key_near = wide_swap(d_key)
+    d_value_near = wide_swap(d_value)
+    grad_kv = ring_sum(
+        strip_rows_grad(
+            [normed_one],
+            normed_one_near,
+            [d_key, d_value],
+            [d_key_near, d_value_near],
+            tbl,
+            strip,
+            4,
+        )
+    )
     grad_key, grad_value = grad_kv[:, :kv_width], grad_kv[:, kv_width:]
+    grad_down = jnp.concatenate([grad_down_a, grad_down_b], axis=0)
+    second_count = hidden - first_count
+    grad_gate = jnp.concatenate(
+        [grad_gate_up_a[:, :first_count], grad_gate_up_b[:, :second_count]], axis=1
+    )
+    grad_up = jnp.concatenate(
+        [grad_gate_up_a[:, first_count:], grad_gate_up_b[:, second_count:]], axis=1
+    )
 
     def strip_rows(weight):
         return lax.dynamic_slice_in_dim(weight, wide_index * strip, strip).astype(F32)
 
     def gain_grad(pairs, gain):
-        local = sum(jnp.sum(strip_rows(w) * g, axis=1) for w, g in pairs)[None, :]
-        local = local + narrow_swap(local, 1)
-        local = local + narrow_swap(local, 2)
-        return local[0] / lax.dynamic_slice_in_dim(gain, wide_index * strip, strip)
-
-    grad_gain_two = gain_grad([(w_gate, grad_gate), (w_up, grad_up)], gain_two)
-    grad_gain_one = gain_grad(
-        [(w_query, grad_query), (w_key, grad_key), (w_value, grad_value)], gain_one
-    )
+        local = sum(jnp.sum(strip_rows(w) * g, axis=1) for w, g in pairs)
+        return local / lax.dynamic_slice_in_dim(gain, wide_index * strip, strip)
+
+    local = jnp.stack(
+        [
+            gain_grad([(w_query, grad_query), (w_key, grad_key), (w_value, grad_value)], gain_one),
+            gain_grad([(w_gate, grad_gate), (w_up, grad_up)], gain_two),
+        ]
+    )
+    local = local + narrow_swap(local, 1)
+    local = local + narrow_swap(local, 2)
+    grad_gain_one, grad_gain_two = local[0], local[1]
     return (
         output,
         grad_tokens,

time: 617 us -> 498 us (0.81)
  Pallas kernels: 39.3 us -> 147 us
  matrix products: 107 us -> 0 us
  local copies, waits for them, and re-layouts: 92.6 us -> 11.8 us
  waiting for transfers between devices: 277 us -> 224 us
  other arithmetic: 32.1 us -> 66.3 us
  starting transfers between devices: 59.3 us -> 41.6 us
    pallas_call x0 -> x19, Pallas kernels: none -> 112 us  [the longest x4 29.5 us: strip_rows_grad(): pl.pallas_call(functools.partial(strip_rows_kernel, len(left), len(left_n...]
    dot_general x42 -> x0, matrix products: 107 us -> none  [dot(): return lax.dot_general(a, b, dims, preferred_element_type=F32)]
    unnamed x144 -> x96, local copies, waits for them, and re-layouts: 43 us -> 3.38 us
    ppermute x18 -> x19, waiting for transfers between devices: 130 us -> 92.1 us  [wide_swap(): lax.ppermute(value, 'wide', [(w, w ^ 1) for w in range(lax.axis_size('wid...]
    dynamic_slice x5 -> x0, local copies, waits for them, and re-layouts: 25 us -> none  [the longest x4 22.7 us: strips(): theirs = lax.dynamic_index_in_dim(cells, 1 - side, 2, keepdims=False)]
    convert_element_type x2 -> x21, other arithmetic: 4.12 us -> 27.4 us  [the longest x14 12.4 us: ring_sum(): carried = total.astype(BF)]
    reshape x4 -> x0, local copies, waits for them, and re-layouts: 15.9 us -> none  [the longest x3 13.8 us: strips(): cells = value.reshape(value.shape[0], turns, 2, strip)]
    ppermute x24 -> x27, starting transfers between devices: 28.9 us -> 15.2 us  [wide_ring(): return lax.ppermute(value, 'wide', pairs)]
  transfers between devices with their start and end apart: 58 -> 63, of which waited for: 27 -> 33; matrix products, arithmetic and copies ran while one was open for 35% -> 13% of each run, Pallas kernels for 4% -> 26%
where the time goes in v2:
time: 498 us; the launch traced here: 492 us
  waiting for transfers between devices  224 us (45%)
  Pallas kernels  147 us (30%)
  other arithmetic  66.3 us (13%)
  starting transfers between devices  41.6 us (8%)
  local copies, waits for them, and re-layouts  11.8 us (2%)
    ppermute x27, waiting for transfers between devices, wide_ring(): return lax.ppermute(value, 'wide', pairs)  126 us
    ppermute x19, waiting for transfers between devices, wide_swap(): lax.ppermute(value, 'wide', [(w, w ^ 1) for w in range(lax.axis_size('wid...  92.1 us
    pallas_call x4, Pallas kernels, strip_rows_grad(): pl.pallas_call(functools.partial(strip_rows_kernel, len(left), len(left_n...  29.5 us
    ppermute x19, starting transfers between devices, wide_swap(): lax.ppermute(value, 'wide', [(w, w ^ 1) for w in range(lax.axis_size('wid...  18.2 us
    pallas_call x3, Pallas kernels, project(): pl.pallas_call(functools.partial(project_kernel, plan), out_shape=[jax.Sh...  16.9 us
    pallas_call x2, Pallas kernels, gated(): pl.pallas_call(gated_kernel, out_shape=[jax.ShapeDtypeStruct((2 * half, c...  16 us
    ppermute x27, starting transfers between devices, wide_ring(): return lax.ppermute(value, 'wide', pairs)  15.2 us
    pallas_call x1, Pallas kernels, attn_bwd(): pl.pallas_call(functools.partial(attn_bwd_kernel, count), out_shape=[jax....  14.9 us
  transfers between devices with their start and end apart: 63, of which 33 were waited for; matrix products, arithmetic and copies ran while one was open for 13% of the time, Pallas kernels for 26%

profile of v2, /device:TPU:0, one launch (start us, length us, event | category | flops | bytes accessed | tf_op | source)
XLA Modules:
  0.0 491.6 jit_solution(9846803674500085831)
XLA Ops:
  29.6 8.5 %inner_grad.1.di_ref = f32[512,1408]{1,0:T(8,128)} custom-call(bf16[512,2048]{1,0:T(8,128)(2,1)} %maximum_select_fusion.x_ref.refs_1_, bf16[1408,2048]{1,0:T(8,128)(2,1)} %refs_1_.4), custom_call_target="tpu_custom_call" | custom-call | flops 4600000000 | tf_op jit(solution)/shard_map/inner_grad/pallas_call | solution.py:423
  59.5 9.0 %collective-permute-done.6.refs_11_.refs_16_ = bf16[512,512]{1,0:T(8,128)(2,1)S(1)} collective-permute-done((bf16[512,512]{1,0:T(8,128)(2,1)}, bf16[512,512]{1,0:T(8,128)(2,1)S(1)}, u32[]{:S(2)}, u32[]{:S(2)}) %collective-permute-start.6) | collective-permute-done | bytes 524320 | tf_op jit(solution)/shard_map/ppermute | solution.py:37
  69.2 10.6 %attn_fwd.1 = (bf16[512,512]{1,0:T(8,128)(2,1)}, f32[4,512]{1,0:T(4,128)}) custom-call(s32[20]{0:T(128)} %pad_add_fusion.2.refs_0_, bf16[512,512]{1,0:T(8,128)(2,1)} %query_proj.1.refs_1_, s32[1,512]{1,0:T(1,128)} %bitcast.27, s32[1,512]{1,0:T(1,128)} %bitcast.25, bf16[512,512]{1,0:T(8,128)(2,1)} %get-tuple-element.97.refs_4_.refs_9_, ...), custom_call_target="tpu_custom_call" | custom-call | flops 5200000000 | tf_op jit(solution)/shard_map/attn_fwd/pallas_call | solution.py:185
  89.7 19.6 %collective-permute-done.9 = bf16[256,2048]{1,0:T(8,128)(2,1)} collective-permute-done((bf16[256,2048]{1,0:T(8,128)(2,1)S(1)}, bf16[256,2048]{1,0:T(8,128)(2,1)}, u32[]{:S(2)}, u32[]{:S(2)}) %collective-permute-start.9) | collective-permute-done | bytes 1048608 | tf_op jit(solution)/shard_map/ppermute | solution.py:37
  119.3 11.2 %collective-permute-done.37.refs_1_ = bf16[512,512]{1,0:T(8,128)(2,1)} collective-permute-done((bf16[512,512]{1,0:T(8,128)(2,1)}, bf16[512,512]{1,0:T(8,128)(2,1)}, u32[]{:S(2)}, u32[]{:S(2)}) %collective-permute-start.37) | collective-permute-done | bytes 524320 | tf_op jit(solution)/shard_map/ppermute | solution.py:37
  131.6 8.3 %gated.2 = (bf16[512,768]{1,0:T(8,128)(2,1)}, bf16[2,512,768]{2,1,0:T(8,128)(2,1)}) custom-call(bf16[256,2048]{1,0:T(8,128)(2,1)} %multiply_convert_fusion.1.own_ref.refs_0_, bf16[256,2048]{1,0:T(8,128)(2,1)} %collective-permute-done.10.other_ref.refs_1_, bf16[2048,1408]{1,0:T(8,128)(2,1)} %wg_ref.5, bf16[2048,1408]{1,0:T(8,128)(2,1)} %wu_ref.5, ...), custom_call_target="tpu_custom_call" | custom-call | flops 4312500224 | tf_op jit(solution)/shard_map/gated/pallas_call | solution.py:376
  139.9 7.7 %gated.3 = (bf16[512,640]{1,0:T(8,128)(2,1)}, bf16[2,512,640]{2,1,0:T(8,128)(2,1)}) custom-call(bf16[256,2048]{1,0:T(8,128)(2,1)} %multiply_convert_fusion.1.own_ref.refs_0_, bf16[256,2048]{1,0:T(8,128)(2,1)} %collective-permute-done.10.other_ref.refs_1_, bf16[2048,1408]{1,0:T(8,128)(2,1)} %wg_ref.5, bf16[2048,1408]{1,0:T(8,128)(2,1)} %wu_ref.5, ...), custom_call_target="tpu_custom_call" | custom-call | flops 4312500224 | tf_op jit(solution)/shard_map/gated/pallas_call | solution.py:376
  147.6 10.8 %back_dense.1 = (bf16[256,2048]{1,0:T(8,128)(2,1)}, bf16[256,2048]{1,0:T(8,128)(2,1)}) custom-call(bf16[2,512,768]{2,1,0:T(8,128)(2,1)} %get-tuple-element.156.first_ref.refs_4_, bf16[2,512,640]{2,1,0:T(8,128)(2,1)} %get-tuple-element.161.second_ref.refs_4_, bf16[2048,1408]{1,0:T(8,128)(2,1)} %wg_ref.5, bf16[2048,1408]{1,0:T(8,128)(2,1)} %wu_ref.5), custom_call_target="tpu_custom_call" | custom-call | flops 6325000192 | tf_op jit(solution)/shard_map/back_dense/pallas_call | solution.py:344
  163.9 14.8 %collective-permute-done.40.refs_1_ = bf16[512,768]{1,0:T(8,128)(2,1)} collective-permute-done((bf16[512,768]{1,0:T(8,128)(2,1)}, bf16[512,768]{1,0:T(8,128)(2,1)}, u32[]{:S(2)}, u32[]{:S(2)}) %collective-permute-start.40) | collective-permute-done | bytes 786464 | tf_op jit(solution)/shard_map/ppermute | solution.py:37
  190.6 8.3 %collective-permute-done.57 = bf16[768,256]{1,0:T(8,128)(2,1)S(1)} collective-permute-done((bf16[768,256]{1,0:T(8,128)(2,1)}, bf16[768,256]{1,0:T(8,128)(2,1)S(1)}, u32[]{:S(2)}, u32[]{:S(2)}) %collective-permute-start.57) | collective-permute-done | bytes 393248 | tf_op jit(solution)/shard_map/ppermute | solution.py:46
  206.3 7.6 %collective-permute-done.58 = bf16[768,256]{1,0:T(8,128)(2,1)} collective-permute-done((bf16[768,256]{1,0:T(8,128)(2,1)}, bf16[768,256]{1,0:T(8,128)(2,1)}, u32[]{:S(2)}, u32[]{:S(2)}) %collective-permute-start.58) | collective-permute-done | bytes 393248 | tf_op jit(solution)/shard_map/ppermute | solution.py:46
  235.0 7.1 %project.4 = (bf16[256,2048]{1,0:T(8,128)(2,1)}, bf16[256,2048]{1,0:T(8,128)(2,1)}) custom-call(bf16[512,768]{1,0:T(8,128)(2,1)} %get-tuple-element.154.refs_0_, bf16[1408,2048]{1,0:T(8,128)(2,1)} %refs_1_.4, bf16[512,640]{1,0:T(8,128)(2,1)} %get-tuple-element.155.refs_2_.refs_0_), custom_call_target="tpu_custom_call" | custom-call | flops 3449999872 | tf_op jit(solution)/shard_map/project/pallas_call | solution.py:316
  249.6 14.9 %attn_bwd.1 = (bf16[512,512]{1,0:T(8,128)(2,1)}, bf16[512,512]{1,0:T(8,128)(2,1)}, bf16[512,512]{1,0:T(8,128)(2,1)}, bf16[512,512]{1,0:T(8,128)(2,1)}, bf16[512,...) custom-call(s32[20]{0:T(128)} %pad_add_fusion.2.refs_0_, ...), custom_call_target="tpu_custom_call" | custom-call | flops 7200000000 | tf_op jit(solution)/shard_map/attn_bwd/pallas_call | solution.py:257
  264.9 9.1 %strip_rows.6 = (bf16[256,1536]{1,0:T(8,128)(2,1)}, bf16[256,1536]{1,0:T(8,128)(2,1)}, bf16[256,1536]{1,0:T(8,128)(2,1)}, bf16[256,1536]{1,0:T(8,128)(2,1)}) custom-call(s32[2,4]{1,0:T(2,128)} %pad_add_fusion.tbl, bf16[256,2048]{1,0:T(8,128)(2,1)} %multiply_convert_fusion.1.own_ref.refs_0_, bf16[256,2048]{1,0:T(8,128)(2,1)} %collective-permute-done.10.other_ref.refs_1_, ...), custom_call_target="tpu_custom_call" | custom-call | flops 4600000000 | tf_op jit(solution)/shard_map/strip_rows/pallas_call | solution.py:525
  285.7 6.8 %collective-permute-done.28.refs_4_ = bf16[512,512]{1,0:T(8,128)(2,1)} collective-permute-done((bf16[512,512]{1,0:T(8,128)(2,1)}, bf16[512,512]{1,0:T(8,128)(2,1)}, u32[]{:S(2)}, u32[]{:S(2)}) %collective-permute-start.28) | collective-permute-done | bytes 524320 | tf_op jit(solution)/shard_map/ppermute | solution.py:37
  308.5 7.3 %collective-permute-done.29 = bf16[256,512]{1,0:T(8,128)(2,1)S(1)} collective-permute-done((bf16[256,512]{1,0:T(8,128)(2,1)}, bf16[256,512]{1,0:T(8,128)(2,1)S(1)}, u32[]{:S(2)}, u32[]{:S(2)}) %collective-permute-start.29) | collective-permute-done | bytes 262176 | tf_op jit(solution)/shard_map/ppermute | solution.py:46
  318.6 10.0 %collective-permute-done.18 = bf16[512,512]{1,0:T(8,128)(2,1)} collective-permute-done((bf16[512,512]{1,0:T(8,128)(2,1)}, bf16[512,512]{1,0:T(8,128)(2,1)}, u32[]{:S(2)}, u32[]{:S(2)}) %collective-permute-start.18) | collective-permute-done | bytes 524320 | tf_op jit(solution)/shard_map/ppermute | solution.py:37
  332.6 7.9 %collective-permute-done.30 = bf16[256,512]{1,0:T(8,128)(2,1)S(1)} collective-permute-done((bf16[256,512]{1,0:T(8,128)(2,1)S(1)}, bf16[256,512]{1,0:T(8,128)(2,1)S(1)}, u32[]{:S(2)}, u32[]{:S(2)}) %collective-permute-start.30) | collective-permute-done | bytes 262176 | tf_op jit(solution)/shard_map/ppermute | solution.py:46
  342.1 8.8 %strip_rows.7 = (bf16[256,1280]{1,0:T(8,128)(2,1)}, bf16[256,1280]{1,0:T(8,128)(2,1)}, bf16[256,1280]{1,0:T(8,128)(2,1)}, bf16[256,1280]{1,0:T(8,128)(2,1)}) custom-call(s32[2,4]{1,0:T(2,128)} %pad_add_fusion.tbl, bf16[256,2048]{1,0:T(8,128)(2,1)} %multiply_convert_fusion.1.own_ref.refs_0_, bf16[256,2048]{1,0:T(8,128)(2,1)} %collective-permute-done.10.other_ref.refs_1_, ...), custom_call_target="tpu_custom_call" | custom-call | flops 4024999936 | tf_op jit(solution)/shard_map/strip_rows/pallas_call | solution.py:525
  350.9 8.0 %collective-permute-done.31 = bf16[256,512]{1,0:T(8,128)(2,1)} collective-permute-done((bf16[256,512]{1,0:T(8,128)(2,1)S(1)}, bf16[256,512]{1,0:T(8,128)(2,1)}, u32[]{:S(2)}, u32[]{:S(2)}) %collective-permute-start.31) | collective-permute-done | bytes 262176 | tf_op jit(solution)/shard_map/ppermute | solution.py:46
  367.1 9.0 %collective-permute-done.52.refs_4_ = bf16[256,1024]{1,0:T(8,128)(2,1)} collective-permute-done((bf16[256,1024]{1,0:T(8,128)(2,1)}, bf16[256,1024]{1,0:T(8,128)(2,1)}, u32[]{:S(2)}, u32[]{:S(2)}) %collective-permute-start.52) | collective-permute-done | bytes 524320 | tf_op jit(solution)/shard_map/ppermute | solution.py:37
  382.2 24.4 %collective-permute-done.23.c_ref = bf16[512,512]{1,0:T(8,128)(2,1)S(1)} collective-permute-done((bf16[512,512]{1,0:T(8,128)(2,1)S(1)}, bf16[512,512]{1,0:T(8,128)(2,1)S(1)}, u32[]{:S(2)}, u32[]{:S(2)}) %collective-permute-start.23) | collective-permute-done | bytes 524320 | tf_op jit(solution)/shard_map/ppermute | solution.py:46
  434.7 6.8 %collective-permute-done.34 = bf16[256,512]{1,0:T(8,128)(2,1)S(1)} collective-permute-done((bf16[256,512]{1,0:T(8,128)(2,1)}, bf16[256,512]{1,0:T(8,128)(2,1)S(1)}, u32[]{:S(2)}, u32[]{:S(2)}) %collective-permute-start.34) | collective-permute-done | bytes 262176 | tf_op jit(solution)/shard_map/ppermute | solution.py:46
  456.1 10.7 %collective-permute-done.49 = bf16[256,1280]{1,0:T(8,128)(2,1)S(1)} collective-permute-done((bf16[256,1280]{1,0:T(8,128)(2,1)S(1)}, bf16[256,1280]{1,0:T(8,128)(2,1)S(1)}, u32[]{:S(2)}, u32[]{:S(2)}) %collective-permute-start.49) | collective-permute-done | bytes 655392 | tf_op jit(solution)/shard_map/ppermute | solution.py:46
  (303 shorter events, 242.6 us)
Async XLA Ops:
  83.7 25.7 %collective-permute-start.9 = (bf16[256,2048]{1,0:T(8,128)(2,1)S(1)}, bf16[256,2048]{1,0:T(8,128)(2,1)}, u32[]{:S(2)}, u32[]{:S(2)}) collective-permute-start(bf16[256,2048]{1,0:T(8,128)(2,1)S(1)} %copy-done.35), channel_id=1, source_target_pairs={{0,4},{4,0},{8,12},{12,8},{16,20},{20,16},{24,28},{28,24},{1,5},{5... | collective-permute-start | bytes 3145736 | tf_op jit(solution)/shard_map/ppermute | solution.py:37
  88.2 25.3 %collective-permute-start.8 = (bf16[256,2048]{1,0:T(8,128)(2,1)S(1)}, bf16[256,2048]{1,0:T(8,128)(2,1)S(1)}, u32[]{:S(2)}, u32[]{:S(2)}) collective-permute-start(bf16[256,2048]{1,0:T(8,128)(2,1)S(1)} %add_convert_fusion.4), channel_id=1, source_target_pairs={{0,2},{1,3},{2,0},{3,1},{4,6},{5,7},{6,4},{7,5},{8,10},{9,11},{10,... | collective-permute-start | bytes 3145736 | tf_op jit(solution)/shard_map/ppermute | solution.py:33
  116.9 44.8 %collective-permute-start.27 = (bf16[256,2048]{1,0:T(8,128)(2,1)}, bf16[256,2048]{1,0:T(8,128)(2,1)}, u32[]{:S(2)}, u32[]{:S(2)}) collective-permute-start(bf16[256,2048]{1,0:T(8,128)(2,1)} %collective-permute-done.9), channel_id=1, source_target_pairs={{0,1},{1,0},{2,3},{3,2},{4,5},{5,4},{6,7},{7,6},{8,9},{9,8},{10,11... | collective-permute-start | bytes 3145736 | tf_op jit(solution)/shard_map/ppermute | solution.py:33
  130.5 27.9 %collective-permute-start.38 = (bf16[256,1024]{1,0:T(8,128)(2,1)}, bf16[256,1024]{1,0:T(8,128)(2,1)}, u32[]{:S(2)}, u32[]{:S(2)}) collective-permute-start(bf16[256,1024]{1,0:T(8,128)(2,1)} %pack.4), channel_id=1, source_target_pairs={{0,4},{4,0},{8,12},{12,8},{16,20},{20,16},{24,28},{28,24},{1,5},{5... | collective-permute-start | bytes 1572872 | tf_op jit(solution)/shard_map/ppermute | solution.py:37
  158.4 28.4 %collective-permute-start.11 = (bf16[256,2048]{1,0:T(8,128)(2,1)}, bf16[256,2048]{1,0:T(8,128)(2,1)}, u32[]{:S(2)}, u32[]{:S(2)}) collective-permute-start(bf16[256,2048]{1,0:T(8,128)(2,1)} %get-tuple-element.124), channel_id=1, source_target_pairs={{0,1},{1,0},{2,3},{3,2},{4,5},{5,4},{6,7},{7,6},{8,9},{9,8},{10,11... | collective-permute-start | bytes 3145736 | tf_op jit(solution)/shard_map/ppermute | solution.py:33
  189.7 32.4 %collective-permute-start.12 = (bf16[256,2048]{1,0:T(8,128)(2,1)}, bf16[256,2048]{1,0:T(8,128)(2,1)}, u32[]{:S(2)}, u32[]{:S(2)}) collective-permute-start(bf16[256,2048]{1,0:T(8,128)(2,1)} %add_convert_fusion.3), channel_id=1, source_target_pairs={{0,2},{1,3},{2,0},{3,1},{4,6},{5,7},{6,4},{7,5},{8,10},{9,11},{10,... | collective-permute-start | bytes 3145736 | tf_op jit(solution)/shard_map/ppermute | solution.py:33
  205.9 58.9 %collective-permute-start.39 = (bf16[256,1024]{1,0:T(8,128)(2,1)}, bf16[256,1024]{1,0:T(8,128)(2,1)}, u32[]{:S(2)}, u32[]{:S(2)}) collective-permute-start(bf16[256,1024]{1,0:T(8,128)(2,1)} %collective-permute-done.38.refs_2_), channel_id=1, source_target_pairs={{0,1},{1,0},{2,3},{3,2},{4,5},{5,4},{6,7},{7,6},{8,9},{9,8},{10,11... | collective-permute-start | bytes 1572872 | tf_op jit(solution)/shard_map/ppermute | solution.py:33
  206.0 58.9 %collective-permute-start.42 = (bf16[2,512,768]{2,1,0:T(8,128)(2,1)}, bf16[2,512,768]{2,1,0:T(8,128)(2,1)}, u32[]{:S(2)}, u32[]{:S(2)}) collective-permute-start(bf16[2,512,768]{2,1,0:T(8,128)(2,1)} %get-tuple-element.156.first_ref.refs_4_), channel_id=1, source_target_pairs={{0,4},{4,0},{8,12},{12,8},{16,20},{20,16},{24,28},{28,24},{1,5},{5... | collective-permute-start | bytes 4718600 | tf_op jit(solution)/shard_map/ppermute | solution.py:37
  215.7 26.4 %collective-permute-start.59 = (bf16[768,256]{1,0:T(8,128)(2,1)}, bf16[768,256]{1,0:T(8,128)(2,1)}, u32[]{:S(2)}, u32[]{:S(2)}) collective-permute-start(bf16[768,256]{1,0:T(8,128)(2,1)} %add_convert_fusion.12), channel_id=1, source_target_pairs={{0,8},{4,12},{8,16},{12,20},{16,24},{20,28},{24,0},{28,4},{1,9},{5... | collective-permute-start | bytes 1179656 | tf_op jit(solution)/shard_map/ppermute | solution.py:46
  274.0 27.6 %collective-permute-start.43 = (bf16[256,1536]{1,0:T(8,128)(2,1)}, bf16[256,1536]{1,0:T(8,128)(2,1)}, u32[]{:S(2)}, u32[]{:S(2)}) collective-permute-start(bf16[256,1536]{1,0:T(8,128)(2,1)} %get-tuple-element.160), channel_id=1, source_target_pairs={{0,8},{4,12},{8,16},{12,20},{16,24},{20,28},{24,0},{28,4},{1,9},{5... | collective-permute-start | bytes 2359304 | tf_op jit(solution)/shard_map/ppermute | solution.py:46
  278.6 62.0 %collective-permute-start.46 = (bf16[2,512,640]{2,1,0:T(8,128)(2,1)}, bf16[2,512,640]{2,1,0:T(8,128)(2,1)}, u32[]{:S(2)}, u32[]{:S(2)}) collective-permute-start(bf16[2,512,640]{2,1,0:T(8,128)(2,1)} %get-tuple-element.161.second_ref.refs_4_), channel_id=1, source_target_pairs={{0,4},{4,0},{8,12},{12,8},{16,20},{20,16},{24,28},{28,24},{1,5},{5... | collective-permute-start | bytes 3932168 | tf_op jit(solution)/shard_map/ppermute | solution.py:37
  280.6 35.4 %collective-permute-start.14 = (bf16[256,2048]{1,0:T(8,128)(2,1)}, bf16[256,2048]{1,0:T(8,128)(2,1)S(1)}, u32[]{:S(2)}, u32[]{:S(2)}) collective-permute-start(bf16[256,2048]{1,0:T(8,128)(2,1)} %get-tuple-element.125), channel_id=1, source_target_pairs={{0,1},{1,0},{2,3},{3,2},{4,5},{5,4},{6,7},{7,6},{8,9},{9,8},{10,11... | collective-permute-start | bytes 3145736 | tf_op jit(solution)/shard_map/ppermute | solution.py:33
  283.5 45.1 %collective-permute-start.18 = (bf16[512,512]{1,0:T(8,128)(2,1)}, bf16[512,512]{1,0:T(8,128)(2,1)}, u32[]{:S(2)}, u32[]{:S(2)}) collective-permute-start(bf16[512,512]{1,0:T(8,128)(2,1)} %get-tuple-element.133), channel_id=1, source_target_pairs={{0,4},{4,0},{8,12},{12,8},{16,20},{20,16},{24,28},{28,24},{1,5},{5... | collective-permute-start | bytes 1572872 | tf_op jit(solution)/shard_map/ppermute | solution.py:37
  292.5 37.7 %collective-permute-start.21 = (bf16[512,512]{1,0:T(8,128)(2,1)}, bf16[512,512]{1,0:T(8,128)(2,1)}, u32[]{:S(2)}, u32[]{:S(2)}) collective-permute-start(bf16[512,512]{1,0:T(8,128)(2,1)} %add_convert_fusion.11), channel_id=1, source_target_pairs={{0,8},{4,12},{8,16},{12,20},{16,24},{20,28},{24,0},{28,4},{1,9},{5... | collective-permute-start | bytes 1572872 | tf_op jit(solution)/shard_map/ppermute | solution.py:46
  315.8 45.1 %collective-permute-start.44 = (bf16[256,1536]{1,0:T(8,128)(2,1)}, bf16[256,1536]{1,0:T(8,128)(2,1)}, u32[]{:S(2)}, u32[]{:S(2)}) collective-permute-start(bf16[256,1536]{1,0:T(8,128)(2,1)} %add_convert_fusion.6), channel_id=1, source_target_pairs={{0,8},{4,12},{8,16},{12,20},{16,24},{20,28},{24,0},{28,4},{1,9},{5... | collective-permute-start | bytes 2359304 | tf_op jit(solution)/shard_map/ppermute | solution.py:46
  328.6 51.0 %collective-permute-start.15 = (bf16[256,2048]{1,0:T(8,128)(2,1)S(1)}, bf16[256,2048]{1,0:T(8,128)(2,1)}, u32[]{:S(2)}, u32[]{:S(2)}) collective-permute-start(bf16[256,2048]{1,0:T(8,128)(2,1)S(1)} %add_convert_fusion.2), channel_id=1, source_target_pairs={{0,2},{1,3},{2,0},{3,1},{4,6},{5,7},{6,4},{7,5},{8,10},{9,11},{10,... | collective-permute-start | bytes 3145736 | tf_op jit(solution)/shard_map/ppermute | solution.py:33
  330.1 33.3 %collective-permute-start.19 = (bf16[512,512]{1,0:T(8,128)(2,1)}, bf16[512,512]{1,0:T(8,128)(2,1)}, u32[]{:S(2)}, u32[]{:S(2)}) collective-permute-start(bf16[512,512]{1,0:T(8,128)(2,1)} %get-tuple-element.134), channel_id=1, source_target_pairs={{0,4},{4,0},{8,12},{12,8},{16,20},{20,16},{24,28},{28,24},{1,5},{5... | collective-permute-start | bytes 1572872 | tf_op jit(solution)/shard_map/ppermute | solution.py:37
  363.5 58.6 %collective-permute-start.45 = (bf16[256,1536]{1,0:T(8,128)(2,1)}, bf16[256,1536]{1,0:T(8,128)(2,1)}, u32[]{:S(2)}, u32[]{:S(2)}) collective-permute-start(bf16[256,1536]{1,0:T(8,128)(2,1)} %add_convert_fusion.5), channel_id=1, source_target_pairs={{0,8},{4,12},{8,16},{12,20},{16,24},{20,28},{24,0},{28,4},{1,9},{5... | collective-permute-start | bytes 2359304 | tf_op jit(solution)/shard_map/ppermute | solution.py:46
  376.0 30.6 %collective-permute-start.23 = (bf16[512,512]{1,0:T(8,128)(2,1)S(1)}, bf16[512,512]{1,0:T(8,128)(2,1)S(1)}, u32[]{:S(2)}, u32[]{:S(2)}) collective-permute-start(bf16[512,512]{1,0:T(8,128)(2,1)S(1)} %add_convert_fusion.9), channel_id=1, source_target_pairs={{0,8},{4,12},{8,16},{12,20},{16,24},{20,28},{24,0},{28,4},{1,9},{5... | collective-permute-start | bytes 1572872 | tf_op jit(solution)/shard_map/ppermute | solution.py:46
  378.5 37.5 %collective-permute-start.53 = (bf16[256,1024]{1,0:T(8,128)(2,1)}, bf16[256,1024]{1,0:T(8,128)(2,1)}, u32[]{:S(2)}, u32[]{:S(2)}) collective-permute-start(bf16[256,1024]{1,0:T(8,128)(2,1)} %collective-permute-done.52.refs_4_), channel_id=1, source_target_pairs={{0,1},{1,0},{2,3},{3,2},{4,5},{5,4},{6,7},{7,6},{8,9},{9,8},{10,11... | collective-permute-start | bytes 1572872 | tf_op jit(solution)/shard_map/ppermute | solution.py:33
  379.6 62.1 %collective-permute-start.48 = (bf16[256,1280]{1,0:T(8,128)(2,1)}, bf16[256,1280]{1,0:T(8,128)(2,1)}, u32[]{:S(2)}, u32[]{:S(2)}) collective-permute-start(bf16[256,1280]{1,0:T(8,128)(2,1)} %add_convert_fusion.8), channel_id=1, source_target_pairs={{0,8},{4,12},{8,16},{12,20},{16,24},{20,28},{24,0},{28,4},{1,9},{5... | collective-permute-start | bytes 1966088 | tf_op jit(solution)/shard_map/ppermute | solution.py:46
  382.2 102.2 %collective-permute-start.16 = (bf16[256,2048]{1,0:T(8,128)(2,1)S(1)}, bf16[256,2048]{1,0:T(8,128)(2,1)}, u32[]{:S(2)}, u32[]{:S(2)}) collective-permute-start(bf16[256,2048]{1,0:T(8,128)(2,1)S(1)} %add_convert_fusion.1), channel_id=1, source_target_pairs={{0,1},{1,0},{2,3},{3,2},{4,5},{5,4},{6,7},{7,6},{8,9},{9,8},{10,11... | collective-permute-start | bytes 3145736 | tf_op jit(solution)/shard_map/ppermute | solution.py:33
  422.1 30.8 %collective-permute-start.24 = (bf16[256,2048]{1,0:T(8,128)(2,1)}, bf16[256,2048]{1,0:T(8,128)(2,1)}, u32[]{:S(2)}, u32[]{:S(2)}) collective-permute-start(bf16[256,2048]{1,0:T(8,128)(2,1)} %get-tuple-element.142), channel_id=1, source_target_pairs={{0,1},{1,0},{2,3},{3,2},{4,5},{5,4},{6,7},{7,6},{8,9},{9,8},{10,11... | collective-permute-start | bytes 3145736 | tf_op jit(solution)/shard_map/ppermute | solution.py:33
  447.2 34.7 %collective-permute-start.56 = (bf16[512,256]{1,0:T(8,128)(2,1)S(1)}, bf16[512,256]{1,0:T(8,128)(2,1)S(1)}, u32[]{:S(2)}, u32[]{:S(2)}) collective-permute-start(bf16[512,256]{1,0:T(8,128)(2,1)S(1)} %add_convert_fusion.16), channel_id=1, source_target_pairs={{0,8},{4,12},{8,16},{12,20},{16,24},{20,28},{24,0},{28,4},{1,9},{5... | collective-permute-start | bytes 786440 | tf_op jit(solution)/shard_map/ppermute | solution.py:46
  (86 other events, 1178.0 us)
